TPU v7x, 256 devices: a whole 4x4x8 slice. The times are simulated.
256 devices in a mesh: seq: 16 (over y, x), chan: 16 (over z, core).
Axes of the slice: x: 4, y: 4, z: 8, core: 2. Of those that a mesh axis runs over, the one named last changes fastest.
Arguments:
- signal: float32 [8192, 4096], P('seq', 'chan'), may hold values from -6 to 6
- filter_taps: float32 [8192, 4096], P('seq', 'chan'), may hold values from -3 to 3
- out_gate: float32 [8192, 4096], P('seq', 'chan'), may hold values from -6 to 6
- skip_gain: float32 [4096], P('chan'), may hold values from -4 to 4
- lengths: int32 [128], replicated, may hold values from 1 to 512, 8192 in all
- row_of_segment: int32 [128], replicated, may hold values from 0 to 127, each once
Outputs:
- mixed: float32 [8192, 4096], P('seq', 'chan')
- pooled: float32 [128, 4096], P('seq', 'chan')
Inputs may be any that keep to these rules, and one draw needn't show every extreme that they name: `lengths`: segments tile the sequence; pooled row r belongs to index r // 8 of seq. `row_of_segment`: each row appears once.
All inputs are finite; a program needn't handle non-finite values.
Results may differ from a plain program's by a relative error of at most 0.000078.
Values sent between devices are 32-bit elements; how exact they have to be, the bound alone decides.
No kernel may reach another device: no remote copies, remote signals or barrier semaphores. Data moves between devices by JAX's collectives and lax.ppermute only.
A program may use at most 64 MiB of HBM per device.

v0:
```python
import math

import jax
import jax.numpy as jnp
from jax import lax
from jax.sharding import PartitionSpec as P

exact_mode = lax.Precision.HIGHEST


def partner_2(value, axis, bit):
    return lax.ppermute(value, axis, [(i, i ^ 1 << bit) for i in range(lax.axis_size(axis))])


def complex_dot(left_re, left_im, right_re, right_im):
    out_re = jnp.dot(left_re, right_re, precision=exact_mode) - jnp.dot(
        left_im, right_im, precision=exact_mode
    )
    out_im = jnp.dot(left_re, right_im, precision=exact_mode) + jnp.dot(
        left_im, right_re, precision=exact_mode
    )
    return (out_re, out_im)


def rotate(real_part, imag_part, phase_angle):
    cosine = jnp.cos(phase_angle)
    sine = jnp.sin(phase_angle)
    return (real_part * cosine - imag_part * sine, real_part * sine + imag_part * cosine)


def local_transform(real_part, imag_part, direction):
    block_rows, columns = real_part.shape
    outer_size = max(
        (divisor for divisor in range(1, math.isqrt(block_rows) + 1) if block_rows % divisor == 0)
    )
    inner_size = block_rows // outer_size
    outer_index = jnp.arange(outer_size, dtype=jnp.int32)
    inner_index = jnp.arange(inner_size, dtype=jnp.int32)
    outer_angle = (
        direction
        * 2.0
        * math.pi
        * (outer_index[:, None] * outer_index[None, :] % outer_size).astype(jnp.float32)
        / outer_size
    )
    twist_angle = (
        direction
        * 2.0
        * math.pi
        * (outer_index[:, None] * inner_index[None, :] % block_rows).astype(jnp.float32)
        / block_rows
    )
    inner_angle = (
        direction
        * 2.0
        * math.pi
        * (inner_index[:, None] * inner_index[None, :] % inner_size).astype(jnp.float32)
        / inner_size
    )
    step_re, step_im = complex_dot(
        jnp.cos(outer_angle),
        jnp.sin(outer_angle),
        real_part.reshape(outer_size, inner_size * columns),
        imag_part.reshape(outer_size, inner_size * columns),
    )
    step_re = step_re.reshape(outer_size, inner_size, columns)
    step_im = step_im.reshape(outer_size, inner_size, columns)
    step_re, step_im = rotate(step_re, step_im, twist_angle[:, :, None])
    inner_cos = jnp.cos(inner_angle)
    inner_sin = jnp.sin(inner_angle)
    out_re = jnp.einsum("sak,at->tsk", step_re, inner_cos, precision=exact_mode) - jnp.einsum(
        "sak,at->tsk", step_im, inner_sin, precision=exact_mode
    )
    out_im = jnp.einsum("sak,at->tsk", step_re, inner_sin, precision=exact_mode) + jnp.einsum(
        "sak,at->tsk", step_im, inner_cos, precision=exact_mode
    )
    return (out_re.reshape(block_rows, columns), out_im.reshape(block_rows, columns))


def bit_reverse(value, levels):
    result = jnp.zeros_like(value)
    for level in range(levels):
        digit = jnp.bitwise_and(jnp.right_shift(value, level), 1)
        result = jnp.bitwise_or(result, jnp.left_shift(digit, levels - 1 - level))
    return result


def spread_pair(values, phase_angle):
    zero_part = jnp.zeros_like(values)
    odd_re, odd_im = rotate(values, zero_part, phase_angle)
    return (values, zero_part, odd_re, odd_im)


def forward_step(state, other, seq_index, level):
    half_span = 1 << level
    upper_side = jnp.bitwise_and(jnp.right_shift(seq_index, level), 1) == 1
    phase_angle = -math.pi * (seq_index % half_span).astype(jnp.float32) / half_span
    result = []
    for slot_pair in range(len(state) // 2):
        own_re, own_im = (state[2 * slot_pair], state[2 * slot_pair + 1])
        far_re, far_im = (other[2 * slot_pair], other[2 * slot_pair + 1])
        diff_re, diff_im = rotate(far_re - own_re, far_im - own_im, phase_angle)
        result.append(jnp.where(upper_side, diff_re, own_re + far_re))
        result.append(jnp.where(upper_side, diff_im, own_im + far_im))
    return tuple(result)


def forward_butterfly(signal, filter_taps):
    seq_count = lax.axis_size("seq")
    levels = seq_count.bit_length() - 1
    seq_index = lax.axis_index("seq")
    top_level = levels - 1
    partner = jnp.bitwise_xor(seq_index, 1 << top_level)
    signal_far, taps_far = partner_2((signal, filter_taps), "seq", top_level)
    own_angle = -math.pi * seq_index.astype(jnp.float32) / seq_count
    far_angle = -math.pi * partner.astype(jnp.float32) / seq_count
    state = spread_pair(signal, own_angle) + spread_pair(filter_taps, own_angle)
    other = spread_pair(signal_far, far_angle) + spread_pair(taps_far, far_angle)
    state = forward_step(state, other, seq_index, top_level)
    for level in range(top_level - 1, -1, -1):
        other = partner_2(
            (state[0], state[1], state[2], state[3], state[4], state[5], state[6], state[7]),
            "seq",
            level,
        )
        state = forward_step(state, other, seq_index, level)
    return state


def inverse_butterfly(even_re, even_im, odd_re, odd_im):
    seq_count = lax.axis_size("seq")
    levels = seq_count.bit_length() - 1
    seq_index = lax.axis_index("seq")
    state = (even_re, even_im, odd_re, odd_im)
    for level in range(levels):
        other = partner_2((state[0], state[1], state[2], state[3]), "seq", level)
        half_span = 1 << level
        upper_side = jnp.bitwise_and(jnp.right_shift(seq_index, level), 1) == 1
        phase_angle = math.pi * (seq_index % half_span).astype(jnp.float32) / half_span
        result = []
        for slot_pair in range(2):
            own_re, own_im = (state[2 * slot_pair], state[2 * slot_pair + 1])
            far_re, far_im = (other[2 * slot_pair], other[2 * slot_pair + 1])
            turned_far = rotate(far_re, far_im, phase_angle)
            turned_own = rotate(own_re, own_im, phase_angle)
            result.append(
                jnp.where(
                    upper_side, 0.5 * (far_re - turned_own[0]), 0.5 * (own_re + turned_far[0])
                )
            )
            result.append(
                jnp.where(
                    upper_side, 0.5 * (far_im - turned_own[1]), 0.5 * (own_im + turned_far[1])
                )
            )
        state = tuple(result)
    block_rows = even_re.shape[0]
    phase_angle = math.pi * seq_index.astype(jnp.float32) / seq_count
    combined = state[0] + jnp.cos(phase_angle) * state[2] - jnp.sin(phase_angle) * state[3]
    return combined / (2.0 * block_rows)


def spectral_convolution(signal, filter_taps, seq_index, seq_count, levels):
    block_rows, channels = signal.shape
    state = forward_butterfly(signal, filter_taps)
    reversed_own = bit_reverse(seq_index, levels)
    positions = jnp.arange(block_rows, dtype=jnp.int32)
    total_len = 2 * seq_count * block_rows
    freq_even = 2 * reversed_own
    freq_odd = freq_even + 1
    even_angle = (
        2.0 * math.pi * (freq_even * positions % total_len).astype(jnp.float32) / total_len
    )[:, None]
    odd_angle = (
        2.0 * math.pi * (freq_odd * positions % total_len).astype(jnp.float32) / total_len
    )[:, None]
    signal_even = rotate(state[0], state[1], -even_angle)
    signal_odd = rotate(state[2], state[3], -odd_angle)
    taps_even = rotate(state[4], state[5], -even_angle)
    taps_odd = rotate(state[6], state[7], -odd_angle)
    joined_re = jnp.concatenate((signal_even[0], signal_odd[0], taps_even[0], taps_odd[0]), axis=1)
    joined_im = jnp.concatenate((signal_even[1], signal_odd[1], taps_even[1], taps_odd[1]), axis=1)
    spec_re, spec_im = local_transform(joined_re, joined_im, -1.0)
    left_re, left_im = (spec_re[:, : 2 * channels], spec_im[:, : 2 * channels])
    right_re, right_im = (spec_re[:, 2 * channels :], spec_im[:, 2 * channels :])
    product_re = left_re * right_re - left_im * right_im
    product_im = left_re * right_im + left_im * right_re
    back_re, back_im = local_transform(product_re, product_im, 1.0)
    even_back = rotate(back_re[:, :channels], back_im[:, :channels], even_angle)
    odd_back = rotate(back_re[:, channels:], back_im[:, channels:], odd_angle)
    return inverse_butterfly(even_back[0], even_back[1], odd_back[0], odd_back[1])


def pool_segments(mixed, lengths, row_of_segment, seq_index, seq_count):
    block_rows = mixed.shape[0]
    owned_rows = lengths.shape[0] // seq_count
    span_ends = jnp.cumsum(lengths)
    span_starts = span_ends - lengths
    tokens = seq_index * block_rows + jnp.arange(block_rows, dtype=jnp.int32)
    inside = (span_starts[None, :] <= tokens[:, None]) & (tokens[:, None] < span_ends[None, :])
    token_row = jnp.sum(jnp.where(inside, row_of_segment[None, :], 0), axis=1)
    wanted = jnp.arange(owned_rows * lax.axis_size("seq"), dtype=jnp.int32)
    member = (token_row[None, :] == wanted[:, None]).astype(jnp.float32)
    sums = lax.psum_scatter(
        jnp.dot(member, mixed, precision=exact_mode), "seq", scatter_dimension=0, tiled=True
    )
    mine = seq_index * owned_rows + jnp.arange(owned_rows, dtype=jnp.int32)
    seg_sizes = jnp.sum(
        jnp.where(row_of_segment[None, :] == mine[:, None], lengths[None, :], 0), axis=1
    )
    return sums / seg_sizes.astype(jnp.float32)[:, None]


def on_device(signal, filter_taps, out_gate, skip_gain, lengths, row_of_segment):
    seq_count = lax.axis_size("seq")
    levels = seq_count.bit_length() - 1
    seq_index = lax.axis_index("seq")
    conv = spectral_convolution(signal, filter_taps, seq_index, seq_count, levels)
    mixed = out_gate * (conv + skip_gain[None, :] * signal)
    pooled = pool_segments(mixed, lengths, row_of_segment, seq_index, seq_count)
    return (mixed, pooled)


def solution(mesh):
    placed = (P("seq", "chan"), P("seq", "chan"), P("seq", "chan"), P("chan"), P(), P())
    return jax.shard_map(
        on_device,
        mesh=mesh,
        in_specs=placed,
        out_specs=(P("seq", "chan"), P("seq", "chan")),
        check_vma=False,
    )
```

profile of v0, /device:TPU:96, one launch (start us, length us, event | category | flops | bytes accessed | tf_op | source)
XLA Modules:
  0.0 579.2 jit_solution(11430512482478350330)
XLA Ops:
  11.9 11.9 %collective-permute-done = f32[512,256]{1,0:T(8,128)S(1)} collective-permute-done((f32[512,256]{1,0:T(8,128)}, f32[512,256]{1,0:T(8,128)S(1)}, u32[]{:S(2)}, u32[]{:S(2)}) %collective-permute-start) | collective-permute-done | bytes 524320 | tf_op jit(solution)/shard_map/ppermute | solution.py:12
  48.0 9.9 %collective-permute-done.2 = f32[512,256]{1,0:T(8,128)S(1)} collective-permute-done((f32[512,256]{1,0:T(8,128)S(1)}, f32[512,256]{1,0:T(8,128)S(1)}, u32[]{:S(2)}, u32[]{:S(2)}) %collective-permute-start.2) | collective-permute-done | bytes 524320 | tf_op jit(solution)/shard_map/ppermute | solution.py:12
  59.4 9.7 %collective-permute-done.14 = f32[512,256]{1,0:T(8,128)S(1)} collective-permute-done((f32[512,256]{1,0:T(8,128)S(1)}, f32[512,256]{1,0:T(8,128)S(1)}, u32[]{:S(2)}, u32[]{:S(2)}) %collective-permute-start.14) | collective-permute-done | bytes 524320 | tf_op jit(solution)/shard_map/ppermute | solution.py:12
  70.4 9.9 %collective-permute-done.15 = f32[512,256]{1,0:T(8,128)S(1)} collective-permute-done((f32[512,256]{1,0:T(8,128)S(1)}, f32[512,256]{1,0:T(8,128)S(1)}, u32[]{:S(2)}, u32[]{:S(2)}) %collective-permute-start.15) | collective-permute-done | bytes 524320 | tf_op jit(solution)/shard_map/ppermute | solution.py:12
  94.6 8.2 %collective-permute-done.8 = f32[512,256]{1,0:T(8,128)S(1)} collective-permute-done((f32[512,256]{1,0:T(8,128)S(1)}, f32[512,256]{1,0:T(8,128)S(1)}, u32[]{:S(2)}, u32[]{:S(2)}) %collective-permute-start.8) | collective-permute-done | bytes 524320 | tf_op jit(solution)/shard_map/ppermute | solution.py:12
  141.9 9.7 %collective-permute-done.9 = f32[512,256]{1,0:T(8,128)S(1)} collective-permute-done((f32[512,256]{1,0:T(8,128)S(1)}, f32[512,256]{1,0:T(8,128)S(1)}, u32[]{:S(2)}, u32[]{:S(2)}) %collective-permute-start.9) | collective-permute-done | bytes 524320 | tf_op jit(solution)/shard_map/ppermute | solution.py:12
  153.4 9.5 %collective-permute-done.22 = f32[512,256]{1,0:T(8,128)S(1)} collective-permute-done((f32[512,256]{1,0:T(8,128)S(1)}, f32[512,256]{1,0:T(8,128)S(1)}, u32[]{:S(2)}, u32[]{:S(2)}) %collective-permute-start.22) | collective-permute-done | bytes 524320 | tf_op jit(solution)/shard_map/ppermute | solution.py:12
  164.4 9.7 %collective-permute-done.23 = f32[512,256]{1,0:T(8,128)S(1)} collective-permute-done((f32[512,256]{1,0:T(8,128)S(1)}, f32[512,256]{1,0:T(8,128)S(1)}, u32[]{:S(2)}, u32[]{:S(2)}) %collective-permute-start.23) | collective-permute-done | bytes 524320 | tf_op jit(solution)/shard_map/ppermute | solution.py:12
  175.9 9.6 %collective-permute-done.5 = f32[512,256]{1,0:T(8,128)S(1)} collective-permute-done((f32[512,256]{1,0:T(8,128)S(1)}, f32[512,256]{1,0:T(8,128)S(1)}, u32[]{:S(2)}, u32[]{:S(2)}) %collective-permute-start.5) | collective-permute-done | bytes 524320 | tf_op jit(solution)/shard_map/ppermute | solution.py:12
  186.9 9.8 %collective-permute-done.6 = f32[512,256]{1,0:T(8,128)S(1)} collective-permute-done((f32[512,256]{1,0:T(8,128)S(1)}, f32[512,256]{1,0:T(8,128)S(1)}, u32[]{:S(2)}, u32[]{:S(2)}) %collective-permute-start.6) | collective-permute-done | bytes 524320 | tf_op jit(solution)/shard_map/ppermute | solution.py:12
  198.4 20.8 %collective-permute-done.11 = f32[512,256]{1,0:T(8,128)S(1)} collective-permute-done((f32[512,256]{1,0:T(8,128)S(1)}, f32[512,256]{1,0:T(8,128)S(1)}, u32[]{:S(2)}, u32[]{:S(2)}) %collective-permute-start.11) | collective-permute-done | bytes 524320 | tf_op jit(solution)/shard_map/ppermute | solution.py:12
  220.6 9.8 %collective-permute-done.12 = f32[512,256]{1,0:T(8,128)S(1)} collective-permute-done((f32[512,256]{1,0:T(8,128)S(1)}, f32[512,256]{1,0:T(8,128)S(1)}, u32[]{:S(2)}, u32[]{:S(2)}) %collective-permute-start.12) | collective-permute-done | bytes 524320 | tf_op jit(solution)/shard_map/ppermute | solution.py:12
  230.7 11.0 %collective-permute-done.19 = f32[512,256]{1,0:T(8,128)S(1)} collective-permute-done((f32[512,256]{1,0:T(8,128)S(1)}, f32[512,256]{1,0:T(8,128)S(1)}, u32[]{:S(2)}, u32[]{:S(2)}) %collective-permute-start.19) | collective-permute-done | bytes 524320 | tf_op jit(solution)/shard_map/ppermute | solution.py:12
  242.8 10.1 %collective-permute-done.24 = f32[512,256]{1,0:T(8,128)S(1)} collective-permute-done((f32[512,256]{1,0:T(8,128)S(1)}, f32[512,256]{1,0:T(8,128)S(1)}, u32[]{:S(2)}, u32[]{:S(2)}) %collective-permute-start.24) | collective-permute-done | bytes 524320 | tf_op jit(solution)/shard_map/ppermute | solution.py:12
  252.9 9.2 %collective-permute-done.25 = f32[512,256]{1,0:T(8,128)S(1)} collective-permute-done((f32[512,256]{1,0:T(8,128)S(1)}, f32[512,256]{1,0:T(8,128)S(1)}, u32[]{:S(2)}, u32[]{:S(2)}) %collective-permute-start.25) | collective-permute-done | bytes 524320 | tf_op jit(solution)/shard_map/ppermute | solution.py:12
  316.6 10.7 %collective-permute-done.26 = f32[512,256]{1,0:T(8,128)S(1)} collective-permute-done((f32[512,256]{1,0:T(8,128)S(1)}, f32[512,256]{1,0:T(8,128)S(1)}, u32[]{:S(2)}, u32[]{:S(2)}) %collective-permute-start.26) | collective-permute-done | bytes 524320 | tf_op jit(solution)/shard_map/ppermute | solution.py:12
  327.4 11.2 %collective-permute-done.27 = f32[512,256]{1,0:T(8,128)S(1)} collective-permute-done((f32[512,256]{1,0:T(8,128)S(1)}, f32[512,256]{1,0:T(8,128)S(1)}, u32[]{:S(2)}, u32[]{:S(2)}) %collective-permute-start.27) | collective-permute-done | bytes 524320 | tf_op jit(solution)/shard_map/ppermute | solution.py:12
  349.9 11.2 %collective-permute-done.35 = f32[512,256]{1,0:T(8,128)S(1)} collective-permute-done((f32[512,256]{1,0:T(8,128)S(1)}, f32[512,256]{1,0:T(8,128)S(1)}, u32[]{:S(2)}, u32[]{:S(2)}) %collective-permute-start.35) | collective-permute-done | bytes 524320 | tf_op jit(solution)/shard_map/ppermute | solution.py:12
  372.4 11.2 %collective-permute-done.29 = f32[512,256]{1,0:T(8,128)} collective-permute-done((f32[512,256]{1,0:T(8,128)S(1)}, f32[512,256]{1,0:T(8,128)}, u32[]{:S(2)}, u32[]{:S(2)}) %collective-permute-start.29) | collective-permute-done | bytes 524320 | tf_op jit(solution)/shard_map/ppermute | solution.py:12
  394.9 8.7 %collective-permute-done.37 = f32[512,256]{1,0:T(8,128)} collective-permute-done((f32[512,256]{1,0:T(8,128)S(1)}, f32[512,256]{1,0:T(8,128)}, u32[]{:S(2)}, u32[]{:S(2)}) %collective-permute-start.37) | collective-permute-done | bytes 524320 | tf_op jit(solution)/shard_map/ppermute | solution.py:12
  420.1 11.2 %collective-permute-done.39 = f32[512,256]{1,0:T(8,128)} collective-permute-done((f32[512,256]{1,0:T(8,128)S(1)}, f32[512,256]{1,0:T(8,128)}, u32[]{:S(2)}, u32[]{:S(2)}) %collective-permute-start.39) | collective-permute-done | bytes 524320 | tf_op jit(solution)/shard_map/ppermute | solution.py:12
  442.4 11.2 %collective-permute-done.33 = f32[512,256]{1,0:T(8,128)} collective-permute-done((f32[512,256]{1,0:T(8,128)S(1)}, f32[512,256]{1,0:T(8,128)}, u32[]{:S(2)}, u32[]{:S(2)}) %collective-permute-start.33) | collective-permute-done | bytes 524320 | tf_op jit(solution)/shard_map/ppermute | solution.py:12
  453.7 11.1 %collective-permute-done.40 = f32[512,256]{1,0:T(8,128)S(1)} collective-permute-done((f32[512,256]{1,0:T(8,128)S(1)}, f32[512,256]{1,0:T(8,128)S(1)}, u32[]{:S(2)}, u32[]{:S(2)}) %collective-permute-start.40) | collective-permute-done | bytes 524320 | tf_op jit(solution)/shard_map/ppermute | solution.py:12
  477.9 92.7 %all-reduce.3.cloned.1.call-done = f32[128,256]{1,0:T(8,128)} async-done(((f32[128,256]{1,0:T(8,128)}), f32[128,256]{1,0:T(8,128)}) %all-reduce.3.cloned.1.call-update) | async-done | bytes 131088
  (162 shorter events, 223.8 us)
Async XLA Ops:
  7.2 563.4 %all-reduce.3.cloned.1.call-start = ((), (), s32[]{:S(2)}) async-start(), calls=%async_computation | async-start | bytes 262144
  37.2 43.1 %collective-permute-start.15 = (f32[512,256]{1,0:T(8,128)S(1)}, f32[512,256]{1,0:T(8,128)S(1)}, u32[]{:S(2)}, u32[]{:S(2)}) collective-permute-start(f32[512,256]{1,0:T(8,128)S(1)} %get-tuple-element.58), channel_id=1, source_target_pairs={{0,64},{16,80},{32,96},{48,112},{64,0},{80,16},{96,32},{112,48},{1... | collective-permute-start | bytes 1572872 | tf_op jit(solution)/shard_map/ppermute | solution.py:12
  37.8 53.8 %collective-permute-start.7 = (f32[512,256]{1,0:T(8,128)S(1)}, f32[512,256]{1,0:T(8,128)S(1)}, u32[]{:S(2)}, u32[]{:S(2)}) collective-permute-start(f32[512,256]{1,0:T(8,128)S(1)} %get-tuple-element.56), channel_id=1, source_target_pairs={{0,64},{16,80},{32,96},{48,112},{64,0},{80,16},{96,32},{112,48},{1... | collective-permute-start | bytes 1572872 | tf_op jit(solution)/shard_map/ppermute | solution.py:12
  46.6 56.2 %collective-permute-start.8 = (f32[512,256]{1,0:T(8,128)S(1)}, f32[512,256]{1,0:T(8,128)S(1)}, u32[]{:S(2)}, u32[]{:S(2)}) collective-permute-start(f32[512,256]{1,0:T(8,128)S(1)} %get-tuple-element.57), channel_id=1, source_target_pairs={{0,64},{16,80},{32,96},{48,112},{64,0},{80,16},{96,32},{112,48},{1... | collective-permute-start | bytes 1572872 | tf_op jit(solution)/shard_map/ppermute | solution.py:12
  57.9 56.2 %collective-permute-start.20 = (f32[512,256]{1,0:T(8,128)S(1)}, f32[512,256]{1,0:T(8,128)S(1)}, u32[]{:S(2)}, u32[]{:S(2)}) collective-permute-start(f32[512,256]{1,0:T(8,128)S(1)} %get-tuple-element.60), channel_id=1, source_target_pairs={{0,64},{16,80},{32,96},{48,112},{64,0},{80,16},{96,32},{112,48},{1... | collective-permute-start | bytes 1572872 | tf_op jit(solution)/shard_map/ppermute | solution.py:12
  69.1 55.0 %collective-permute-start.21 = (f32[512,256]{1,0:T(8,128)S(1)}, f32[512,256]{1,0:T(8,128)S(1)}, u32[]{:S(2)}, u32[]{:S(2)}) collective-permute-start(f32[512,256]{1,0:T(8,128)S(1)} %get-tuple-element.61), channel_id=1, source_target_pairs={{0,64},{16,80},{32,96},{48,112},{64,0},{80,16},{96,32},{112,48},{1... | collective-permute-start | bytes 1572872 | tf_op jit(solution)/shard_map/ppermute | solution.py:12
  80.3 47.1 %collective-permute-start.3 = (f32[512,256]{1,0:T(8,128)S(1)}, f32[512,256]{1,0:T(8,128)S(1)}, u32[]{:S(2)}, u32[]{:S(2)}) collective-permute-start(f32[512,256]{1,0:T(8,128)S(1)} %get-tuple-element.41), channel_id=1, source_target_pairs={{0,32},{16,48},{32,0},{48,16},{64,96},{80,112},{96,64},{112,80},{1... | collective-permute-start | bytes 1572872 | tf_op jit(solution)/shard_map/ppermute | solution.py:12
  91.6 36.4 %collective-permute-start.4 = (f32[512,256]{1,0:T(8,128)S(1)}, f32[512,256]{1,0:T(8,128)S(1)}, u32[]{:S(2)}, u32[]{:S(2)}) collective-permute-start(f32[512,256]{1,0:T(8,128)S(1)} %get-tuple-element.40), channel_id=1, source_target_pairs={{0,32},{16,48},{32,0},{48,16},{64,96},{80,112},{96,64},{112,80},{1... | collective-permute-start | bytes 1572872 | tf_op jit(solution)/shard_map/ppermute | solution.py:12
  128.0 34.9 %collective-permute-start.22 = (f32[512,256]{1,0:T(8,128)S(1)}, f32[512,256]{1,0:T(8,128)S(1)}, u32[]{:S(2)}, u32[]{:S(2)}) collective-permute-start(f32[512,256]{1,0:T(8,128)S(1)} %get-tuple-element.53), channel_id=1, source_target_pairs={{0,32},{16,48},{32,0},{48,16},{64,96},{80,112},{96,64},{112,80},{1... | collective-permute-start | bytes 1572872 | tf_op jit(solution)/shard_map/ppermute | solution.py:12
  131.5 42.7 %collective-permute-start.23 = (f32[512,256]{1,0:T(8,128)S(1)}, f32[512,256]{1,0:T(8,128)S(1)}, u32[]{:S(2)}, u32[]{:S(2)}) collective-permute-start(f32[512,256]{1,0:T(8,128)S(1)} %get-tuple-element.52), channel_id=1, source_target_pairs={{0,32},{16,48},{32,0},{48,16},{64,96},{80,112},{96,64},{112,80},{1... | collective-permute-start | bytes 1572872 | tf_op jit(solution)/shard_map/ppermute | solution.py:12
  132.1 53.4 %collective-permute-start.5 = (f32[512,256]{1,0:T(8,128)S(1)}, f32[512,256]{1,0:T(8,128)S(1)}, u32[]{:S(2)}, u32[]{:S(2)}) collective-permute-start(f32[512,256]{1,0:T(8,128)S(1)} %get-tuple-element.39), channel_id=1, source_target_pairs={{0,16},{16,0},{32,48},{48,32},{64,80},{80,64},{96,112},{112,96},{1... | collective-permute-start | bytes 1572872 | tf_op jit(solution)/shard_map/ppermute | solution.py:12
  140.4 56.3 %collective-permute-start.6 = (f32[512,256]{1,0:T(8,128)S(1)}, f32[512,256]{1,0:T(8,128)S(1)}, u32[]{:S(2)}, u32[]{:S(2)}) collective-permute-start(f32[512,256]{1,0:T(8,128)S(1)} %get-tuple-element.38), channel_id=1, source_target_pairs={{0,16},{16,0},{32,48},{48,32},{64,80},{80,64},{96,112},{112,96},{1... | collective-permute-start | bytes 1572872 | tf_op jit(solution)/shard_map/ppermute | solution.py:12
  151.7 79.0 %collective-permute-start.18 = (f32[512,256]{1,0:T(8,128)S(1)}, f32[512,256]{1,0:T(8,128)S(1)}, u32[]{:S(2)}, u32[]{:S(2)}) collective-permute-start(f32[512,256]{1,0:T(8,128)S(1)} %get-tuple-element.47), channel_id=1, source_target_pairs={{0,16},{16,0},{32,48},{48,32},{64,80},{80,64},{96,112},{112,96},{1... | collective-permute-start | bytes 1572872 | tf_op jit(solution)/shard_map/ppermute | solution.py:12
  162.9 56.3 %collective-permute-start.11 = (f32[512,256]{1,0:T(8,128)S(1)}, f32[512,256]{1,0:T(8,128)S(1)}, u32[]{:S(2)}, u32[]{:S(2)}) collective-permute-start(f32[512,256]{1,0:T(8,128)S(1)} %get-tuple-element.43), channel_id=1, source_target_pairs={{0,16},{16,0},{32,48},{48,32},{64,80},{80,64},{96,112},{112,96},{1... | collective-permute-start | bytes 1572872 | tf_op jit(solution)/shard_map/ppermute | solution.py:12
  174.1 56.3 %collective-permute-start.12 = (f32[512,256]{1,0:T(8,128)S(1)}, f32[512,256]{1,0:T(8,128)S(1)}, u32[]{:S(2)}, u32[]{:S(2)}) collective-permute-start(f32[512,256]{1,0:T(8,128)S(1)} %get-tuple-element.42), channel_id=1, source_target_pairs={{0,16},{16,0},{32,48},{48,32},{64,80},{80,64},{96,112},{112,96},{1... | collective-permute-start | bytes 1572872 | tf_op jit(solution)/shard_map/ppermute | solution.py:12
  185.5 56.2 %collective-permute-start.19 = (f32[512,256]{1,0:T(8,128)S(1)}, f32[512,256]{1,0:T(8,128)S(1)}, u32[]{:S(2)}, u32[]{:S(2)}) collective-permute-start(f32[512,256]{1,0:T(8,128)S(1)} %get-tuple-element.46), channel_id=1, source_target_pairs={{0,16},{16,0},{32,48},{48,32},{64,80},{80,64},{96,112},{112,96},{1... | collective-permute-start | bytes 1572872 | tf_op jit(solution)/shard_map/ppermute | solution.py:12
  196.7 56.2 %collective-permute-start.24 = (f32[512,256]{1,0:T(8,128)S(1)}, f32[512,256]{1,0:T(8,128)S(1)}, u32[]{:S(2)}, u32[]{:S(2)}) collective-permute-start(f32[512,256]{1,0:T(8,128)S(1)} %get-tuple-element.51), channel_id=1, source_target_pairs={{0,16},{16,0},{32,48},{48,32},{64,80},{80,64},{96,112},{112,96},{1... | collective-permute-start | bytes 1572872 | tf_op jit(solution)/shard_map/ppermute | solution.py:12
  219.2 43.0 %collective-permute-start.25 = (f32[512,256]{1,0:T(8,128)S(1)}, f32[512,256]{1,0:T(8,128)S(1)}, u32[]{:S(2)}, u32[]{:S(2)}) collective-permute-start(f32[512,256]{1,0:T(8,128)S(1)} %get-tuple-element.50), channel_id=1, source_target_pairs={{0,16},{16,0},{32,48},{48,32},{64,80},{80,64},{96,112},{112,96},{1... | collective-permute-start | bytes 1572872 | tf_op jit(solution)/shard_map/ppermute | solution.py:12
  314.6 35.2 %collective-permute-start.34 = (f32[512,256]{1,0:T(8,128)S(1)}, f32[512,256]{1,0:T(8,128)S(1)}, u32[]{:S(2)}, u32[]{:S(2)}) collective-permute-start(f32[512,256]{1,0:T(8,128)S(1)} %get-tuple-element.31), channel_id=1, source_target_pairs={{0,16},{16,0},{32,48},{48,32},{64,80},{80,64},{96,112},{112,96},{1... | collective-permute-start | bytes 1572872 | tf_op jit(solution)/shard_map/ppermute | solution.py:12
  316.1 45.0 %collective-permute-start.35 = (f32[512,256]{1,0:T(8,128)S(1)}, f32[512,256]{1,0:T(8,128)S(1)}, u32[]{:S(2)}, u32[]{:S(2)}) collective-permute-start(f32[512,256]{1,0:T(8,128)S(1)} %get-tuple-element.30), channel_id=1, source_target_pairs={{0,16},{16,0},{32,48},{48,32},{64,80},{80,64},{96,112},{112,96},{1... | collective-permute-start | bytes 1572872 | tf_op jit(solution)/shard_map/ppermute | solution.py:12
  341.0 42.6 %collective-permute-start.29 = (f32[512,256]{1,0:T(8,128)S(1)}, f32[512,256]{1,0:T(8,128)}, u32[]{:S(2)}, u32[]{:S(2)}) collective-permute-start(f32[512,256]{1,0:T(8,128)S(1)} %get-tuple-element.28), channel_id=1, source_target_pairs={{0,32},{16,48},{32,0},{48,16},{64,96},{80,112},{96,64},{112,80},{1... | collective-permute-start | bytes 1572872 | tf_op jit(solution)/shard_map/ppermute | solution.py:12
  363.8 39.8 %collective-permute-start.37 = (f32[512,256]{1,0:T(8,128)S(1)}, f32[512,256]{1,0:T(8,128)}, u32[]{:S(2)}, u32[]{:S(2)}) collective-permute-start(f32[512,256]{1,0:T(8,128)S(1)} %get-tuple-element.37), channel_id=1, source_target_pairs={{0,32},{16,48},{32,0},{48,16},{64,96},{80,112},{96,64},{112,80},{1... | collective-permute-start | bytes 1572872 | tf_op jit(solution)/shard_map/ppermute | solution.py:12
  411.0 42.7 %collective-permute-start.33 = (f32[512,256]{1,0:T(8,128)S(1)}, f32[512,256]{1,0:T(8,128)}, u32[]{:S(2)}, u32[]{:S(2)}) collective-permute-start(f32[512,256]{1,0:T(8,128)S(1)} %get-tuple-element.24), channel_id=1, source_target_pairs={{0,128},{16,144},{32,160},{48,176},{64,192},{80,208},{96,224},{112... | collective-permute-start | bytes 1572872 | tf_op jit(solution)/shard_map/ppermute | solution.py:12
  434.9 38.1 %collective-permute-start.41 = (f32[512,256]{1,0:T(8,128)S(1)}, f32[512,256]{1,0:T(8,128)}, u32[]{:S(2)}, u32[]{:S(2)}) collective-permute-start(f32[512,256]{1,0:T(8,128)S(1)} %get-tuple-element.33), channel_id=1, source_target_pairs={{0,128},{16,144},{32,160},{48,176},{64,192},{80,208},{96,224},{112... | collective-permute-start | bytes 1572872 | tf_op jit(solution)/shard_map/ppermute | solution.py:12
  (31 other events, 768.6 us)
Sparse Core Ops, SparseCore 0:
  476.5 93.9 all-reduce.2
where the time goes:
time: 589 us; the launch traced here: 579 us
  waiting for transfers between devices  425 us (72%)
  starting transfers between devices  67.9 us (12%)
  matrix products  28.7 us (5%)
  other arithmetic  24.9 us (4%)
  between operations  17.1 us (3%)
  local copies, waits for them, and re-layouts  15.3 us (3%)
    ppermute x42, waiting for transfers between devices, partner_2(): lax.ppermute(value, axis, [(i, i ^ 1 << bit) for i in range(lax.axis_size...  332 us
    unnamed x2, waiting for transfers between devices  92.7 us
    ppermute x42, starting transfers between devices, partner_2(): lax.ppermute(value, axis, [(i, i ^ 1 << bit) for i in range(lax.axis_size...  67.9 us
  transfers between devices with their start and end apart: 43, of which 36 were waited for; matrix products, arithmetic and copies ran while one was open for 2% of the time, Pallas kernels for 0%

commit v1 on v0

v1 whole, which is shorter than its diff:
```python
import functools
import math

import jax
import jax.numpy as jnp
import numpy as np
from jax import lax
from jax.experimental import pallas as pl
from jax.experimental.pallas import tpu as pltpu
from jax.sharding import PartitionSpec as P


LANES = 128
INTERPRET = False
bf16 = jnp.bfloat16
f32 = jnp.float32


def split_const(value):
    hi = value.astype(bf16)
    return hi, (value - hi.astype(np.float64)).astype(bf16)


@functools.lru_cache(None)
def tables(seq_count, subs):
    rows = seq_count * subs
    total = rows * LANES
    t1 = np.array([device * subs + sub for sub in range(subs) for device in range(seq_count)], np.float64)
    k1 = np.arange(rows, dtype=np.float64)
    t2 = np.arange(LANES, dtype=np.float64)
    first = -2.0 * math.pi * (k1[:, None] + 0.25) * t1[None, :] / rows
    first = np.concatenate([np.cos(first), np.sin(first)], 0)
    hi, lo = split_const(first)
    first3 = np.concatenate([hi, lo, hi], 1)
    twist = -2.0 * math.pi * (k1[:, None] + 0.25) * t2[None, :] / total
    twist = np.stack([np.cos(twist), np.sin(twist)]).astype(np.float32)
    angle = 2.0 * math.pi * (np.outer(t2, t2) % LANES) / LANES
    cos, sin = np.cos(angle), np.sin(angle)
    forward = np.block([[cos, -sin], [sin, cos]])
    hi, lo = split_const(forward)
    forward3 = np.concatenate([hi, hi, lo], 0)
    hi, lo = split_const(forward.T / total)
    inverse3 = np.concatenate([hi, hi, lo], 0)
    last = 2.0 * math.pi * t1[:, None] * (k1[None, :] + 0.25) / rows
    hi, lo = split_const(np.concatenate([np.cos(last), -np.sin(last)], 1))
    last3 = np.concatenate([hi, lo, hi], 1)
    return first3, twist, forward3, inverse3, last3


def split(value):
    hi = value.astype(bf16)
    lo = (value - hi.astype(f32)).astype(bf16)
    return hi, lo


def mm(left, right):
    return lax.dot_general(left, right, (((1,), (0,)), ((), ())), preferred_element_type=f32)


def turn_kernel(signal, taps, gate, skip, out, *, seq_count, group, subs):
    at_start = lax.axis_index("seq") == 0
    for sub in range(subs):
        rows = slice(sub * LANES, (sub + 1) * LANES)
        for which, ref in enumerate((signal, taps, gate)):
            value = ref[rows, :]
            if which == 1 and sub == 0:
                place = lax.broadcasted_iota(jnp.int32, value.shape, 0)
                value = value + jnp.where((place == 0) & at_start, skip[...], 0.0)
            base = (sub * 3 + which) * group
            out[:, base : base + group, :] = value.T.reshape(seq_count, group, LANES)


def conv_kernel(
    taken, lengths, row_of, first3, twist, forward3, inverse3, last3, out, conv, *, seq_count, group, subs
):
    rows = seq_count * subs
    per = 3 * subs * group
    twist_re, twist_im = twist[0], twist[1]
    pair = 2

    def gather(which, channel):
        parts = []
        for sub in range(subs):
            start = (sub * 3 + which) * group + channel
            parts.append(taken[pl.ds(start, seq_count, stride=per), :])
        return jnp.concatenate(parts, 0)

    for block in range(group // pair):
        turned = []
        for channel in range(block * pair, (block + 1) * pair):
            both = jnp.concatenate([gather(0, channel), gather(1, channel)], 1)
            hi, lo = split(both)
            stage = mm(first3[...], jnp.concatenate([hi, hi, lo], 0))
            for side in range(2):
                lanes = slice(side * LANES, (side + 1) * LANES)
                re, im = stage[:rows, lanes], stage[rows:, lanes]
                turned.append(
                    jnp.concatenate([re * twist_re - im * twist_im, re * twist_im + im * twist_re], 1)
                )
        hi, lo = split(jnp.concatenate(turned, 0))
        spec = mm(jnp.concatenate([hi, lo, hi], 1), forward3[...])
        products = []
        for at in range(pair):
            left = spec[(2 * at) * rows : (2 * at + 1) * rows]
            right = spec[(2 * at + 1) * rows : (2 * at + 2) * rows]
            left_re, left_im = left[:, :LANES], left[:, LANES:]
            right_re, right_im = right[:, :LANES], right[:, LANES:]
            products.append(
                jnp.concatenate(
                    [left_re * right_re - left_im * right_im, left_re * right_im + left_im * right_re], 1
                )
            )
        hi, lo = split(jnp.concatenate(products, 0))
        back = mm(jnp.concatenate([hi, lo, hi], 1), inverse3[...])
        untwisted = []
        for at in range(pair):
            re, im = back[at * rows : (at + 1) * rows, :LANES], back[at * rows : (at + 1) * rows, LANES:]
            untwisted.append(
                jnp.concatenate([re * twist_re + im * twist_im, im * twist_re - re * twist_im], 0)
            )
        hi, lo = split(jnp.concatenate(untwisted, 1))
        result = mm(last3[...], jnp.concatenate([hi, hi, lo], 0))
        for at in range(pair):
            channel = block * pair + at
            for sub in range(subs):
                conv[pl.ds(sub * group + channel, seq_count, stride=subs * group), :] = result[
                    sub * seq_count : (sub + 1) * seq_count, at * LANES : (at + 1) * LANES
                ]

    segs = lengths.shape[1]
    owned = segs // seq_count
    seg_len = lengths[...].astype(f32)
    seg_at = lax.broadcasted_iota(jnp.int32, (segs, segs), 1)
    hit = row_of[...] == lax.broadcasted_iota(jnp.int32, (segs, segs), 0)
    which_seg = jnp.sum(jnp.where(hit, seg_at, 0).astype(f32), axis=1, keepdims=True)
    row_len = jnp.sum(jnp.where(hit, seg_len, 0.0), axis=1, keepdims=True)
    row_start = jnp.sum(jnp.where(seg_at.astype(f32) < which_seg, seg_len, 0.0), axis=1, keepdims=True)
    row_end = row_start + row_len
    token = lax.broadcasted_iota(jnp.int32, (segs, 2 * LANES), 1).astype(f32)
    acc = jnp.zeros((segs, 2 * group), f32)
    for device in range(seq_count):
        for step in range(subs // 2):
            halves = []
            for sub in (2 * step, 2 * step + 1):
                base = (device * subs + sub) * group
                from_row = device * per + (sub * 3 + 2) * group
                mixed = conv[base : base + group, :] * taken[from_row : from_row + group, :]
                out[device, sub * group : (sub + 1) * group, :] = mixed
                halves.append(mixed)
            hi, lo = split(jnp.concatenate(halves, 1))
            here = token + float((device * subs + 2 * step) * LANES)
            member = jnp.where((here >= row_start) & (here < row_end), 1.0, 0.0).astype(bf16)
            acc = acc + lax.dot_general(
                member,
                jnp.concatenate([hi, lo], 0),
                (((1,), (1,)), ((), ())),
                preferred_element_type=f32,
            )
    pooled = (acc[:, :group] + acc[:, group:]) / row_len
    pooled = jnp.concatenate([pooled, jnp.zeros((segs, LANES - group), f32)], 1)
    shift = lax.rem(lax.axis_index("seq"), LANES // group) * group
    pooled = pltpu.roll(pooled, shift, 1)
    out[:, subs * group :, :] = pooled.reshape(seq_count, owned, LANES)


def back_kernel(taken, mixed, pooled, *, seq_count, group, subs):
    channels = seq_count * group
    for sub in range(subs):
        block = taken[:, sub * group : (sub + 1) * group, :].reshape(channels, LANES)
        mixed[sub * LANES : (sub + 1) * LANES, :] = block.T
    per_lane = LANES // group
    for half in range(channels // LANES):
        total = taken[half * per_lane, subs * group :, :]
        for at in range(half * per_lane + 1, (half + 1) * per_lane):
            total = total + taken[at, subs * group :, :]
        pooled[:, half * LANES : (half + 1) * LANES] = total


def on_device(signal, filter_taps, out_gate, skip_gain, lengths, row_of_segment):
    seq_count = lax.axis_size("seq")
    block_rows, channels = signal.shape
    group = channels // seq_count
    subs = block_rows // LANES
    segs = lengths.shape[0]
    owned = segs // seq_count
    sizes = dict(seq_count=seq_count, group=group, subs=subs)
    sent = pl.pallas_call(
        functools.partial(turn_kernel, **sizes),
        out_shape=jax.ShapeDtypeStruct((seq_count, 3 * subs * group, LANES), f32),
        interpret=INTERPRET,
        name="turn",
    )(signal, filter_taps, out_gate, skip_gain.reshape(1, channels))
    taken = lax.all_to_all(sent, "seq", 0, 0)
    consts = [jnp.asarray(table) for table in tables(seq_count, subs)]
    mixed_sent = pl.pallas_call(
        functools.partial(conv_kernel, **sizes),
        out_shape=jax.ShapeDtypeStruct((seq_count, subs * group + owned, LANES), f32),
        scratch_shapes=[pltpu.VMEM((seq_count * subs * group, LANES), f32)],
        interpret=INTERPRET,
        name="conv",
    )(
        taken.reshape(seq_count * 3 * subs * group, LANES),
        lengths.reshape(1, segs),
        row_of_segment.reshape(1, segs),
        *consts,
    )
    back = lax.all_to_all(mixed_sent, "seq", 0, 0)
    return pl.pallas_call(
        functools.partial(back_kernel, **sizes),
        out_shape=(
            jax.ShapeDtypeStruct((block_rows, channels), f32),
            jax.ShapeDtypeStruct((owned, channels), f32),
        ),
        interpret=INTERPRET,
        name="back",
    )(back)


def solution(mesh):
    placed = (P("seq", "chan"), P("seq", "chan"), P("seq", "chan"), P("chan"), P(), P())
    return jax.shard_map(
        on_device,
        mesh=mesh,
        in_specs=placed,
        out_specs=(P("seq", "chan"), P("seq", "chan")),
        check_vma=False,
    )
```

time: 589 us -> 61.3 us (0.10); the launches traced: 579 us -> 60.9 us
  waiting for transfers between devices: 425 us -> 0 us
  starting transfers between devices: 67.9 us -> 0 us
  blocking collectives: 0 us -> 45.3 us
  matrix products: 28.7 us -> 0 us
  other arithmetic: 24.9 us -> 0 us
  between operations: 17.1 us -> 0.63 us
  local copies, waits for them, and re-layouts: 15.3 us -> 0 us
  Pallas kernels: 0 us -> 15 us
    ppermute x42 -> x0, waiting for transfers between devices: 332 us -> none  [partner_2(): lax.ppermute(value, axis, [(i, i ^ 1 << bit) for i in range(lax.axis_size...]
    unnamed x2 -> x0, waiting for transfers between devices: 92.7 us -> none
    ppermute x42 -> x0, starting transfers between devices: 67.9 us -> none  [partner_2(): lax.ppermute(value, axis, [(i, i ^ 1 << bit) for i in range(lax.axis_size...]
    all_to_all x0 -> x2, blocking collectives: none -> 45.3 us  [the longest x1 29.9 us: on_device(): taken = lax.all_to_all(sent, 'seq', 0, 0)]
    dot_general x17 -> x0, matrix products: 28.7 us -> none  [the longest x2 4.68 us: complex_dot(): jnp.dot(left_re, right_im, precision=exact_mode)]
    pallas_call x0 -> x3, Pallas kernels: none -> 15 us  [the longest x1 9.97 us: on_device(): pl.pallas_call(functools.partial(conv_kernel, **sizes), out_shape=jax.Sha...]
    select_n x16 -> x0, other arithmetic: 10.7 us -> none  [the longest x10 3.81 us: forward_step(): result.append(jnp.where(upper_side, diff_im, own_im + far_im))]
    reshape x4 -> x0, local copies, waits for them, and re-layouts: 6.51 us -> none  [the longest x2 4.57 us: local_transform(): imag_part.reshape(outer_size, inner_size * columns)]
  transfers between devices with their start and end apart: 43 -> 0, of which waited for: 36 -> 0; matrix products, arithmetic and copies ran while one was open for 2% -> 0% of each run, Pallas kernels for 0% -> 0%
where the time goes in v1:
time: 61.3 us; the launch traced here: 60.9 us
  blocking collectives  45.3 us (74%)
  Pallas kernels  15 us (24%)
  between operations  0.63 us (1%)
    all_to_all x1, blocking collectives, on_device(): taken = lax.all_to_all(sent, 'seq', 0, 0)  29.9 us
    all_to_all x1, blocking collectives, on_device(): back = lax.all_to_all(mixed_sent, 'seq', 0, 0)  15.4 us
    pallas_call x1, Pallas kernels, on_device(): pl.pallas_call(functools.partial(conv_kernel, **sizes), out_shape=jax.Sha...  9.97 us
    pallas_call x1, Pallas kernels, on_device(): pl.pallas_call(functools.partial(turn_kernel, **sizes), out_shape=jax.Sha...  2.98 us
    pallas_call x1, Pallas kernels, on_device(): pl.pallas_call(functools.partial(back_kernel, **sizes), out_shape=(jax.Sh...  2.06 us

profile of v1, /device:TPU:96, one launch (start us, length us, event | category | flops | bytes accessed | tf_op | source)
XLA Modules:
  0.0 60.9 jit_solution(14958388891586287185)
XLA Ops:
  0.6 3.0 %turn.1 = f32[16,192,128]{2,1,0:T(8,128)} custom-call(f32[512,256]{1,0:T(8,128)} %signal.1, f32[512,256]{1,0:T(8,128)} %taps.1, f32[512,256]{1,0:T(8,128)} %gate.1, f32[1,256]{1,0:T(1,128)} %bitcast.5), custom_call_target="tpu_custom_call" | custom-call | tf_op jit(solution)/shard_map/turn/pallas_call | solution.py:187
  3.6 29.9 %all_to_all.10 = f32[16,192,128]{2,1,0:T(8,128)} all-to-all(f32[16,192,128]{2,1,0:T(8,128)} %turn.1), channel_id=1, replica_groups=mesh['seq'=16,'chan'=16] {'seq'}, dimensions={0} | all-to-all | bytes 3145728 | tf_op jit(solution)/shard_map/all_to_all | solution.py:193
  33.5 10.0 %conv.1 = f32[16,72,128]{2,1,0:T(8,128)} custom-call(f32[3072,128]{1,0:T(8,128)} %bitcast.4, s32[1,128]{1,0:T(1,128)} %bitcast.6, s32[1,128]{1,0:T(1,128)} %bitcast.7, bf16[128,192]{1,0:T(8,128)(2,1)} %constant.10.clone.first3, f32[2,64,128]{2,1,0:T(8,128)} %constant.11.clone.twist, bf16[768,256]{1,0:T(8,128)(2,1)} %constant.12.clone.forward3, ...), custom_call_target="tpu_custom_call" | custom-call | tf_op jit(solution)/shard_map/conv/pallas_call | solution.py:195
  43.5 15.4 %all_to_all.11.taken = f32[16,72,128]{2,1,0:T(8,128)} all-to-all(f32[16,72,128]{2,1,0:T(8,128)} %conv.1), channel_id=1, replica_groups=mesh['seq'=16,'chan'=16] {'seq'}, dimensions={0} | all-to-all | bytes 1179648 | tf_op jit(solution)/shard_map/all_to_all | solution.py:207
  58.9 2.1 %back.1 = (f32[512,256]{1,0:T(8,128)}, f32[8,256]{1,0:T(8,128)}) custom-call(f32[16,72,128]{2,1,0:T(8,128)} %all_to_all.11.taken), custom_call_target="tpu_custom_call" | custom-call | tf_op jit(solution)/shard_map/back/pallas_call | solution.py:208

commit v2 on v1

--- a/solution.py
+++ b/solution.py
@@ -186,25 +186,28 @@
     sizes = dict(seq_count=seq_count, group=group, subs=subs)
     sent = pl.pallas_call(
         functools.partial(turn_kernel, **sizes),
-        out_shape=jax.ShapeDtypeStruct((seq_count, 3 * subs * group, LANES), f32),
+        out_shape=pltpu.VMEM((seq_count, 3 * subs * group, LANES), f32),
         interpret=INTERPRET,
         name="turn",
     )(signal, filter_taps, out_gate, skip_gain.reshape(1, channels))
     taken = lax.all_to_all(sent, "seq", 0, 0)
+    taken = taken.reshape(seq_count * 3 * subs * group, LANES)
+    taken = pltpu.with_memory_space_constraint(taken, pltpu.VMEM)
     consts = [jnp.asarray(table) for table in tables(seq_count, subs)]
     mixed_sent = pl.pallas_call(
         functools.partial(conv_kernel, **sizes),
-        out_shape=jax.ShapeDtypeStruct((seq_count, subs * group + owned, LANES), f32),
+        out_shape=pltpu.VMEM((seq_count, subs * group + owned, LANES), f32),
         scratch_shapes=[pltpu.VMEM((seq_count * subs * group, LANES), f32)],
         interpret=INTERPRET,
         name="conv",
     )(
-        taken.reshape(seq_count * 3 * subs * group, LANES),
+        taken,
         lengths.reshape(1, segs),
         row_of_segment.reshape(1, segs),
         *consts,
     )
     back = lax.all_to_all(mixed_sent, "seq", 0, 0)
+    back = pltpu.with_memory_space_constraint(back, pltpu.VMEM)
     return pl.pallas_call(
         functools.partial(back_kernel, **sizes),
         out_shape=(

time: 61.3 us -> 56.4 us (0.920)
  Pallas kernels: 15 us -> 11.5 us
  blocking collectives: 45.3 us -> 44 us
    pallas_call x2, Pallas kernels: 13 us -> 10.5 us  [the longest x1 8.71 us: on_device(): pl.pallas_call(functools.partial(conv_kernel, **sizes), out_shape=pltpu.V...]
    pallas_call x1, Pallas kernels: 2.06 us -> 1 us  [on_device(): pl.pallas_call(functools.partial(back_kernel, **sizes), out_shape=(jax.Sh...]
    all_to_all x1, blocking collectives: 15.4 us -> 14.4 us  [on_device(): back = lax.all_to_all(mixed_sent, 'seq', 0, 0)]
where the time goes in v2:
time: 56.4 us; the launch traced here: 56.2 us
  blocking collectives  44 us (78%)
  Pallas kernels  11.5 us (20%)
  between operations  0.64 us (1%)
    all_to_all x1, blocking collectives, on_device(): taken = lax.all_to_all(sent, 'seq', 0, 0)  29.6 us
    all_to_all x1, blocking collectives, on_device(): back = lax.all_to_all(mixed_sent, 'seq', 0, 0)  14.4 us
    pallas_call x1, Pallas kernels, on_device(): pl.pallas_call(functools.partial(conv_kernel, **sizes), out_shape=pltpu.V...  8.71 us
    pallas_call x1, Pallas kernels, on_device(): pl.pallas_call(functools.partial(turn_kernel, **sizes), out_shape=pltpu.V...  1.82 us

profile of v2, /device:TPU:96, one launch (start us, length us, event | category | flops | bytes accessed | tf_op | source)
XLA Modules:
  0.0 56.2 jit_solution(8683730741166067589)
XLA Ops:
  0.6 1.8 %turn.1 = f32[16,192,128]{2,1,0:T(8,128)S(1)} custom-call(f32[512,256]{1,0:T(8,128)} %signal.1, f32[512,256]{1,0:T(8,128)} %taps.1, f32[512,256]{1,0:T(8,128)} %gate.1, f32[1,256]{1,0:T(1,128)} %bitcast.5), custom_call_target="tpu_custom_call" | custom-call | tf_op jit(solution)/shard_map/turn/pallas_call | solution.py:187
  2.5 29.6 %all_to_all.10 = f32[16,192,128]{2,1,0:T(8,128)S(1)} all-to-all(f32[16,192,128]{2,1,0:T(8,128)S(1)} %turn.1), channel_id=1, replica_groups=mesh['seq'=16,'chan'=16] {'seq'}, dimensions={0} | all-to-all | bytes 3145728 | tf_op jit(solution)/shard_map/all_to_all | solution.py:193
  32.1 8.7 %conv.1 = f32[16,72,128]{2,1,0:T(8,128)S(1)} custom-call(f32[3072,128]{1,0:T(8,128)S(1)} %bitcast.4, s32[1,128]{1,0:T(1,128)} %bitcast.6, s32[1,128]{1,0:T(1,128)} %bitcast.7, bf16[128,192]{1,0:T(8,128)(2,1)} %constant.10.clone.first3, f32[2,64,128]{2,1,0:T(8,128)} %constant.11.clone.twist, bf16[768,256]{1,0:T(8,128)(2,1)} %constant.12.clone.forward3, ...), custom_call_target="tpu_custom_call" | custom-call | tf_op jit(solution)/shard_map/conv/pallas_call | solution.py:197
  40.8 14.4 %all_to_all.11.taken = f32[16,72,128]{2,1,0:T(8,128)S(1)} all-to-all(f32[16,72,128]{2,1,0:T(8,128)S(1)} %conv.1), channel_id=1, replica_groups=mesh['seq'=16,'chan'=16] {'seq'}, dimensions={0} | all-to-all | bytes 1179648 | tf_op jit(solution)/shard_map/all_to_all | solution.py:209
  55.2 1.0 %back.1 = (f32[512,256]{1,0:T(8,128)}, f32[8,256]{1,0:T(8,128)}) custom-call(f32[16,72,128]{2,1,0:T(8,128)S(1)} %all_to_all.11.taken), custom_call_target="tpu_custom_call" | custom-call | tf_op jit(solution)/shard_map/back/pallas_call | solution.py:211

commit v3 on v2

--- a/solution.py
+++ b/solution.py
@@ -11,6 +11,8 @@
 
 
 LANES = 128
+FWD = 4
+INV = 4
 INTERPRET = False
 bf16 = jnp.bfloat16
 f32 = jnp.float32
@@ -71,12 +73,11 @@
 
 
 def conv_kernel(
-    taken, lengths, row_of, first3, twist, forward3, inverse3, last3, out, conv, *, seq_count, group, subs
+    taken, lengths, row_of, first3, twist, forward3, inverse3, last3, out, conv, turned, product, *, seq_count, group, subs
 ):
     rows = seq_count * subs
     per = 3 * subs * group
     twist_re, twist_im = twist[0], twist[1]
-    pair = 2
 
     def gather(which, channel):
         parts = []
@@ -85,47 +86,57 @@
             parts.append(taken[pl.ds(start, seq_count, stride=per), :])
         return jnp.concatenate(parts, 0)
 
-    for block in range(group // pair):
-        turned = []
-        for channel in range(block * pair, (block + 1) * pair):
-            both = jnp.concatenate([gather(0, channel), gather(1, channel)], 1)
-            hi, lo = split(both)
-            stage = mm(first3[...], jnp.concatenate([hi, hi, lo], 0))
-            for side in range(2):
-                lanes = slice(side * LANES, (side + 1) * LANES)
-                re, im = stage[:rows, lanes], stage[rows:, lanes]
-                turned.append(
-                    jnp.concatenate([re * twist_re - im * twist_im, re * twist_im + im * twist_re], 1)
-                )
-        hi, lo = split(jnp.concatenate(turned, 0))
-        spec = mm(jnp.concatenate([hi, lo, hi], 1), forward3[...])
-        products = []
-        for at in range(pair):
+    for channel in range(group):
+        both = jnp.concatenate([gather(0, channel), gather(1, channel)], 1)
+        hi, lo = split(both)
+        stage = mm(first3[...], jnp.concatenate([hi, hi, lo], 0))
+        for side in range(2):
+            lanes = slice(side * LANES, (side + 1) * LANES)
+            re, im = stage[:rows, lanes], stage[rows:, lanes]
+            at = slice((2 * channel + side) * rows, (2 * channel + side + 1) * rows)
+            for half, value in enumerate((re * twist_re - im * twist_im, re * twist_im + im * twist_re)):
+                lanes_out = slice(half * LANES, (half + 1) * LANES)
+                hi, lo = split(value)
+                turned[at, lanes_out] = hi
+                turned[at, 2 * LANES + half * LANES : 2 * LANES + (half + 1) * LANES] = lo
+
+    def three(ref, at, table):
+        hi, lo = ref[at, : 2 * LANES], ref[at, 2 * LANES :]
+        high = table[: 2 * LANES, :]
+        return mm(hi, high) + mm(lo, high) + mm(hi, table[4 * LANES :, :])
+
+    for block in range(group // FWD):
+        spec = three(turned, slice(block * FWD * 2 * rows, (block + 1) * FWD * 2 * rows), forward3)
+        for at in range(FWD):
+            channel = block * FWD + at
             left = spec[(2 * at) * rows : (2 * at + 1) * rows]
             right = spec[(2 * at + 1) * rows : (2 * at + 2) * rows]
             left_re, left_im = left[:, :LANES], left[:, LANES:]
             right_re, right_im = right[:, :LANES], right[:, LANES:]
-            products.append(
-                jnp.concatenate(
-                    [left_re * right_re - left_im * right_im, left_re * right_im + left_im * right_re], 1
+            products = (left_re * right_re - left_im * right_im, left_re * right_im + left_im * right_re)
+            here = slice(channel * rows, (channel + 1) * rows)
+            for half, value in enumerate(products):
+                hi, lo = split(value)
+                product[here, half * LANES : (half + 1) * LANES] = hi
+                product[here, (2 + half) * LANES : (3 + half) * LANES] = lo
+
+    for block in range(group // INV):
+        back = three(product, slice(block * INV * rows, (block + 1) * INV * rows), inverse3)
+        for pair in range(INV // 2):
+            values = []
+            for at in (2 * pair, 2 * pair + 1):
+                re, im = back[at * rows : (at + 1) * rows, :LANES], back[at * rows : (at + 1) * rows, LANES:]
+                values.append(
+                    jnp.concatenate([re * twist_re + im * twist_im, im * twist_re - re * twist_im], 0)
                 )
-            )
-        hi, lo = split(jnp.concatenate(products, 0))
-        back = mm(jnp.concatenate([hi, lo, hi], 1), inverse3[...])
-        untwisted = []
-        for at in range(pair):
-            re, im = back[at * rows : (at + 1) * rows, :LANES], back[at * rows : (at + 1) * rows, LANES:]
-            untwisted.append(
-                jnp.concatenate([re * twist_re + im * twist_im, im * twist_re - re * twist_im], 0)
-            )
-        hi, lo = split(jnp.concatenate(untwisted, 1))
-        result = mm(last3[...], jnp.concatenate([hi, hi, lo], 0))
-        for at in range(pair):
-            channel = block * pair + at
-            for sub in range(subs):
-                conv[pl.ds(sub * group + channel, seq_count, stride=subs * group), :] = result[
-                    sub * seq_count : (sub + 1) * seq_count, at * LANES : (at + 1) * LANES
-                ]
+            hi, lo = split(jnp.concatenate(values, 1))
+            result = mm(last3[...], jnp.concatenate([hi, hi, lo], 0))
+            for at in range(2):
+                channel = block * INV + pair * 2 + at
+                for sub in range(subs):
+                    conv[pl.ds(sub * group + channel, seq_count, stride=subs * group), :] = result[
+                        sub * seq_count : (sub + 1) * seq_count, at * LANES : (at + 1) * LANES
+                    ]
 
     segs = lengths.shape[1]
     owned = segs // seq_count
@@ -135,8 +146,11 @@
     which_seg = jnp.sum(jnp.where(hit, seg_at, 0).astype(f32), axis=1, keepdims=True)
     row_len = jnp.sum(jnp.where(hit, seg_len, 0.0), axis=1, keepdims=True)
     row_start = jnp.sum(jnp.where(seg_at.astype(f32) < which_seg, seg_len, 0.0), axis=1, keepdims=True)
-    row_end = row_start + row_len
-    token = lax.broadcasted_iota(jnp.int32, (segs, 2 * LANES), 1).astype(f32)
+    token = lax.broadcasted_iota(jnp.int32, (segs, 2 * LANES), 1)
+    past_start = token - row_start.astype(jnp.int32)
+    to_end = (row_len.astype(jnp.int32) - 1 - past_start).astype(jnp.int16)
+    past_start = past_start.astype(jnp.int16)
+    one, zero = jnp.ones((segs, 2 * LANES), bf16), jnp.zeros((segs, 2 * LANES), bf16)
     acc = jnp.zeros((segs, 2 * group), f32)
     for device in range(seq_count):
         for step in range(subs // 2):
@@ -148,8 +162,10 @@
                 out[device, sub * group : (sub + 1) * group, :] = mixed
                 halves.append(mixed)
             hi, lo = split(jnp.concatenate(halves, 1))
-            here = token + float((device * subs + 2 * step) * LANES)
-            member = jnp.where((here >= row_start) & (here < row_end), 1.0, 0.0).astype(bf16)
+            offset = (device * subs + 2 * step) * LANES
+            member = jnp.where(
+                (past_start >= jnp.int16(-offset)) & (to_end >= jnp.int16(offset)), one, zero
+            )
             acc = acc + lax.dot_general(
                 member,
                 jnp.concatenate([hi, lo], 0),
@@ -197,7 +213,11 @@
     mixed_sent = pl.pallas_call(
         functools.partial(conv_kernel, **sizes),
         out_shape=pltpu.VMEM((seq_count, subs * group + owned, LANES), f32),
-        scratch_shapes=[pltpu.VMEM((seq_count * subs * group, LANES), f32)],
+        scratch_shapes=[
+            pltpu.VMEM((seq_count * subs * group, LANES), f32),
+            pltpu.VMEM((2 * group * seq_count * subs, 4 * LANES), bf16),
+            pltpu.VMEM((group * seq_count * subs, 4 * LANES), bf16),
+        ],
         interpret=INTERPRET,
         name="conv",
     )(

time: 56.4 us -> 54.3 us (0.963)
  Pallas kernels: 11.5 us -> 9.34 us
    pallas_call x1, Pallas kernels: 8.71 us -> 6.53 us  [on_device(): pl.pallas_call(functools.partial(conv_kernel, **sizes), out_shape=pltpu.V...]
where the time goes in v3:
time: 54.3 us; the launch traced here: 54.1 us
  blocking collectives  44.1 us (81%)
  Pallas kernels  9.34 us (17%)
  between operations  0.64 us (1%)
    all_to_all x1, blocking collectives, on_device(): taken = lax.all_to_all(sent, 'seq', 0, 0)  29.6 us
    all_to_all x1, blocking collectives, on_device(): back = lax.all_to_all(mixed_sent, 'seq', 0, 0)  14.5 us
    pallas_call x1, Pallas kernels, on_device(): pl.pallas_call(functools.partial(conv_kernel, **sizes), out_shape=pltpu.V...  6.53 us
    pallas_call x1, Pallas kernels, on_device(): pl.pallas_call(functools.partial(turn_kernel, **sizes), out_shape=pltpu.V...  1.82 us

profile of v3, /device:TPU:96, one launch (start us, length us, event | category | flops | bytes accessed | tf_op | source)
XLA Modules:
  0.0 54.1 jit_solution(5732842753064144987)
XLA Ops:
  0.6 1.8 %turn.1 = f32[16,192,128]{2,1,0:T(8,128)S(1)} custom-call(f32[512,256]{1,0:T(8,128)} %signal.1, f32[512,256]{1,0:T(8,128)} %taps.1, f32[512,256]{1,0:T(8,128)} %gate.1, f32[1,256]{1,0:T(1,128)} %bitcast.5), custom_call_target="tpu_custom_call" | custom-call | tf_op jit(solution)/shard_map/turn/pallas_call | solution.py:203
  2.5 29.6 %all_to_all.10 = f32[16,192,128]{2,1,0:T(8,128)S(1)} all-to-all(f32[16,192,128]{2,1,0:T(8,128)S(1)} %turn.1), channel_id=1, replica_groups=mesh['seq'=16,'chan'=16] {'seq'}, dimensions={0} | all-to-all | bytes 3145728 | tf_op jit(solution)/shard_map/all_to_all | solution.py:209
  32.1 6.5 %conv.1 = f32[16,72,128]{2,1,0:T(8,128)S(1)} custom-call(f32[3072,128]{1,0:T(8,128)S(1)} %bitcast.4, s32[1,128]{1,0:T(1,128)} %bitcast.6, s32[1,128]{1,0:T(1,128)} %bitcast.7, bf16[128,192]{1,0:T(8,128)(2,1)} %constant.10.clone.first3, f32[2,64,128]{2,1,0:T(8,128)} %constant.11.clone.twist, bf16[768,256]{1,0:T(8,128)(2,1)} %constant.12.clone.forward3, ...), custom_call_target="tpu_custom_call" | custom-call | tf_op jit(solution)/shard_map/conv/pallas_call | solution.py:213
  38.6 14.5 %all_to_all.11.taken = f32[16,72,128]{2,1,0:T(8,128)S(1)} all-to-all(f32[16,72,128]{2,1,0:T(8,128)S(1)} %conv.1), channel_id=1, replica_groups=mesh['seq'=16,'chan'=16] {'seq'}, dimensions={0} | all-to-all | bytes 1179648 | tf_op jit(solution)/shard_map/all_to_all | solution.py:229
  53.1 1.0 %back.1 = (f32[512,256]{1,0:T(8,128)}, f32[8,256]{1,0:T(8,128)}) custom-call(f32[16,72,128]{2,1,0:T(8,128)S(1)} %all_to_all.11.taken), custom_call_target="tpu_custom_call" | custom-call | tf_op jit(solution)/shard_map/back/pallas_call | solution.py:231

commit v4 on v3

v4 whole, which is shorter than its diff:
```python
import functools
import math

import jax
import jax.numpy as jnp
import numpy as np
from jax import lax
from jax.experimental import pallas as pl
from jax.experimental.pallas import tpu as pltpu
from jax.sharding import PartitionSpec as P


LANES = 128
VMEM_LIMIT = 24 << 20
FWD = 8
ACC = 2
INV = 4
INTERPRET = False
bf16 = jnp.bfloat16
f32 = jnp.float32


def split_const(value):
    hi = value.astype(bf16)
    return hi, (value - hi.astype(np.float64)).astype(bf16)


@functools.lru_cache(None)
def tables(seq_count, subs):
    rows = seq_count * subs
    total = rows * LANES
    t1 = np.array([device * subs + sub for sub in range(subs) for device in range(seq_count)], np.float64)
    k1 = np.arange(rows, dtype=np.float64)
    t2 = np.arange(LANES, dtype=np.float64)
    first = -2.0 * math.pi * (k1[:, None] + 0.25) * t1[None, :] / rows
    hi, lo = split_const(np.concatenate([np.cos(first), np.sin(first)], 0))
    first3 = np.concatenate([hi, lo, hi, np.zeros_like(hi)], 1)
    angle = 2.0 * math.pi * (np.outer(t2, t2) % LANES) / LANES
    cos, sin = np.cos(angle), np.sin(angle)
    forward = np.block([[cos, -sin], [sin, cos]])
    last = 2.0 * math.pi * t1[:, None] * (k1[None, :] + 0.25) / rows
    last_hi, last_lo = split_const(np.concatenate([np.cos(last), -np.sin(last)], 1))
    twist = -2.0 * math.pi * (k1[:, None] + 0.25) * t2[None, :] / total
    twist = np.concatenate([np.cos(twist), np.sin(twist)], 1)
    high, middle = split_const(twist)
    low = (twist - high.astype(np.float64) - middle.astype(np.float64)).astype(bf16)
    parts = [
        *split_const(forward),
        *split_const(forward.T / total),
        first3,
        np.concatenate([last_hi, last_lo], 1),
        np.concatenate([last_hi, np.zeros_like(last_hi)], 1),
        high,
        middle,
        low,
    ]
    return np.concatenate(parts, 0)


def split(value):
    hi = value.astype(bf16)
    lo = (value - hi.astype(f32)).astype(bf16)
    return hi, lo


def mm(left, right):
    return lax.dot_general(left, right, (((1,), (0,)), ((), ())), preferred_element_type=f32)


def turn_kernel(
    signal, taps, gate, skip, lengths, row_of, consts, out, bounds, sizes, table,
    big, row, ints, sems, small_sems,
    *, seq_count, group, subs
):
    small = (
        pltpu.make_async_copy(lengths, ints.at[0], small_sems.at[0]),
        pltpu.make_async_copy(row_of, ints.at[1], small_sems.at[1]),
        pltpu.make_async_copy(skip, row, small_sems.at[2]),
    )
    for copy in small:
        copy.start()
    constant = pltpu.make_async_copy(consts, table, small_sems.at[3])
    large = []
    for which, ref in enumerate((signal, taps, gate)):
        for sub in range(subs):
            rows = pl.ds(sub * LANES, LANES)
            at = which * subs + sub
            large.append(pltpu.make_async_copy(ref.at[rows, :], big.at[at], sems.at[at]))
            large[-1].start()
    constant.start()
    for copy in small:
        copy.wait()

    segs = ints.shape[2]
    seg_len = jnp.broadcast_to(ints[0].astype(f32), (segs, segs)).T
    seg_row = jnp.broadcast_to(ints[1].astype(f32), (segs, segs)).T
    seg_at = lax.broadcasted_iota(jnp.int32, (segs, segs), 0).astype(f32)
    hit = seg_row == lax.broadcasted_iota(jnp.int32, (segs, segs), 1).astype(f32)
    which_seg = jnp.sum(jnp.where(hit, seg_at, 0.0), axis=0, keepdims=True)
    row_len = jnp.sum(jnp.where(hit, seg_len, 0.0), axis=0, keepdims=True)
    row_start = jnp.sum(jnp.where(seg_at < which_seg, seg_len, 0.0), axis=0, keepdims=True)
    bounds[...] = jnp.broadcast_to(row_start, bounds.shape)
    sizes[...] = jnp.broadcast_to(row_len, sizes.shape)

    at_start = lax.axis_index("seq") == 0
    for which in range(3):
        for sub in range(subs):
            large[which * subs + sub].wait()
        for sub in range(subs):
            value = big[which * subs + sub]
            if which == 1 and sub == 0:
                place = lax.broadcasted_iota(jnp.int32, value.shape, 0)
                value = value + jnp.where((place == 0) & at_start, row[...], 0.0)
            base = (sub * 3 + which) * group
            out[:, base : base + group, :] = value.T.reshape(seq_count, group, LANES)
    constant.wait()


def conv_kernel(
    taken, bounds, sizes, table, out, conv, turned, product, unturned, spread, *, seq_count, group, subs
):
    rows = seq_count * subs
    per = 3 * subs * group
    wide = 2 * LANES

    def tabled(at, count, lanes=wide):
        return table[at : at + count, :lanes]

    at = 4 * wide
    first3 = tabled(at, 2 * rows, 3 * rows)
    at += 2 * rows
    last3 = jnp.concatenate([tabled(at, rows), tabled(at + rows, rows, LANES)], 1)
    at += 2 * rows
    twist = tabled(at, rows).astype(f32) + tabled(at + rows, rows).astype(f32)
    twist = twist + tabled(at + 2 * rows, rows).astype(f32)
    twist_re, twist_im = twist[:, :LANES], twist[:, LANES:]

    pitch = 2 * subs * group + 1
    for device in range(seq_count):
        for sub in range(subs):
            for which in range(2):
                base = device * pitch + (sub * 2 + which) * group
                from_row = device * per + (sub * 3 + which) * group
                spread[base : base + group, :] = taken[from_row : from_row + group, :]

    def gather(which, channel):
        parts = []
        for sub in range(subs):
            start = (sub * 2 + which) * group + channel
            parts.append(spread[pl.ds(start, seq_count, stride=pitch), :])
        return jnp.concatenate(parts, 0)

    for channel in range(group):
        both = jnp.concatenate([gather(0, channel), gather(1, channel)], 1)
        hi, lo = split(both)
        stage = mm(first3, jnp.concatenate([hi, hi, lo], 0))
        for side in range(2):
            lanes = slice(side * LANES, (side + 1) * LANES)
            re, im = stage[:rows, lanes], stage[rows:, lanes]
            at = slice((2 * channel + side) * rows, (2 * channel + side + 1) * rows)
            for half, value in enumerate((re * twist_re - im * twist_im, re * twist_im + im * twist_re)):
                lanes_out = slice(half * LANES, (half + 1) * LANES)
                hi, lo = split(value)
                turned[at, lanes_out] = hi
                turned[at, 2 * LANES + half * LANES : 2 * LANES + (half + 1) * LANES] = lo

    def three(ref, at, base):
        high, low = tabled(base, wide), tabled(base + wide, wide)
        return mm(jnp.concatenate([ref[at, :], ref[at, :wide]], 1), jnp.concatenate([high, high, low], 0))

    for block in range(group // FWD):
        spec = three(turned, slice(block * FWD * 2 * rows, (block + 1) * FWD * 2 * rows), 0)
        for at in range(FWD):
            channel = block * FWD + at
            left = spec[(2 * at) * rows : (2 * at + 1) * rows]
            right = spec[(2 * at + 1) * rows : (2 * at + 2) * rows]
            left_re, left_im = left[:, :LANES], left[:, LANES:]
            right_re, right_im = right[:, :LANES], right[:, LANES:]
            products = (left_re * right_re - left_im * right_im, left_re * right_im + left_im * right_re)
            here = slice(channel * rows, (channel + 1) * rows)
            for half, value in enumerate(products):
                hi, lo = split(value)
                product[here, half * LANES : (half + 1) * LANES] = hi
                product[here, (2 + half) * LANES : (3 + half) * LANES] = lo

    for block in range(group // INV):
        back = three(product, slice(block * INV * rows, (block + 1) * INV * rows), 2 * wide)
        for at in range(INV):
            channel = block * INV + at
            lanes = slice(channel % 2 * LANES, (channel % 2 + 1) * LANES)
            re, im = back[at * rows : (at + 1) * rows, :LANES], back[at * rows : (at + 1) * rows, LANES:]
            values = (re * twist_re + im * twist_im, im * twist_re - re * twist_im)
            for half, value in enumerate(values):
                hi, lo = split(value)
                base = channel // 2 * 4 * rows + half * rows
                unturned[base : base + rows, lanes] = hi
                unturned[base + 2 * rows : base + 3 * rows, lanes] = lo

    for pair in range(group // 2):
        hi = unturned[pair * 4 * rows : pair * 4 * rows + 2 * rows, :]
        lo = unturned[pair * 4 * rows + 2 * rows : (pair + 1) * 4 * rows, :]
        result = mm(last3, jnp.concatenate([hi, hi, lo], 0))
        for at in range(2):
            for sub in range(subs):
                start = sub * group + pair * 2 + at
                conv[pl.ds(start, seq_count, stride=subs * group + 1), :] = result[
                    sub * seq_count : (sub + 1) * seq_count, at * LANES : (at + 1) * LANES
                ]

    segs = sizes.shape[1]
    owned = segs // seq_count
    past_start = lax.broadcasted_iota(jnp.int32, (wide, segs), 0) - bounds[:1, :].astype(jnp.int32)
    to_end = (sizes[:1, :].astype(jnp.int32) - 1 - past_start).astype(jnp.int16)
    past_start = past_start.astype(jnp.int16)
    one, zero = jnp.ones((wide, segs), bf16), jnp.zeros((wide, segs), bf16)
    sums = [jnp.zeros((2 * group, segs), f32) for _ in range(ACC)]
    for device in range(seq_count):
        for step in range(subs // 2):
            halves = []
            for sub in (2 * step, 2 * step + 1):
                base = device * (subs * group + 1) + sub * group
                from_row = device * per + (sub * 3 + 2) * group
                mixed = conv[base : base + group, :] * taken[from_row : from_row + group, :]
                out[device, sub * group : (sub + 1) * group, :] = mixed
                halves.append(mixed)
            hi, lo = split(jnp.concatenate(halves, 1))
            offset = (device * subs + 2 * step) * LANES
            member = jnp.where(
                (past_start >= jnp.int16(-offset)) & (to_end >= jnp.int16(offset)), one, zero
            )
            which = (device * (subs // 2) + step) % ACC
            sums[which] = sums[which] + mm(jnp.concatenate([hi, lo], 0), member)
    acc = sum(sums[1:], sums[0])
    pooled = (acc[:group] + acc[group:]) / sizes[:group, :]
    pooled = jnp.concatenate([pooled, jnp.zeros((LANES - group, segs), f32)], 0).T
    shift = lax.rem(lax.axis_index("seq"), LANES // group) * group
    pooled = pltpu.roll(pooled, shift, 1)
    out[:, subs * group :, :] = pooled.reshape(seq_count, owned, LANES)


def back_kernel(taken, mixed, pooled, *, seq_count, group, subs):
    channels = seq_count * group
    for sub in range(subs):
        block = taken[:, sub * group : (sub + 1) * group, :].reshape(channels, LANES)
        mixed[sub * LANES : (sub + 1) * LANES, :] = block.T
    per_lane = LANES // group
    for half in range(channels // LANES):
        total = taken[half * per_lane, subs * group :, :]
        for at in range(half * per_lane + 1, (half + 1) * per_lane):
            total = total + taken[at, subs * group :, :]
        pooled[:, half * LANES : (half + 1) * LANES] = total


def in_vmem(value):
    return pltpu.with_memory_space_constraint(value, pltpu.VMEM)


def on_device(signal, filter_taps, out_gate, skip_gain, lengths, row_of_segment):
    seq_count = lax.axis_size("seq")
    block_rows, channels = signal.shape
    group = channels // seq_count
    subs = block_rows // LANES
    segs = lengths.shape[0]
    owned = segs // seq_count
    sizes = dict(seq_count=seq_count, group=group, subs=subs)
    anywhere = pl.BlockSpec(memory_space=pltpu.HBM)
    consts = jnp.asarray(tables(seq_count, subs))
    sent, bounds, row_sizes, table = pl.pallas_call(
        functools.partial(turn_kernel, **sizes),
        in_specs=[anywhere] * 7,
        out_shape=(
            pltpu.VMEM((seq_count, 3 * subs * group, LANES), f32),
            pltpu.VMEM((2 * group, segs), f32),
            pltpu.VMEM((2 * group, segs), f32),
            pltpu.VMEM(consts.shape, bf16),
        ),
        scratch_shapes=[
            pltpu.VMEM((3 * subs, LANES, channels), f32),
            pltpu.VMEM((1, channels), f32),
            pltpu.VMEM((2, 1, segs), jnp.int32),
            pltpu.SemaphoreType.DMA((3 * subs,)),
            pltpu.SemaphoreType.DMA((4,)),
        ],
        interpret=INTERPRET,
        name="turn",
        compiler_params=pltpu.CompilerParams(vmem_limit_bytes=VMEM_LIMIT),
    )(
        *(
            pltpu.with_memory_space_constraint(value, pltpu.HBM)
            for value in (
                signal,
                filter_taps,
                out_gate,
                skip_gain.reshape(1, channels),
                lengths.reshape(1, segs),
                row_of_segment.reshape(1, segs),
                consts,
            )
        )
    )
    taken = lax.all_to_all(sent, "seq", 0, 0)
    taken = in_vmem(taken.reshape(seq_count * 3 * subs * group, LANES))
    mixed_sent = pl.pallas_call(
        functools.partial(conv_kernel, **sizes),
        out_shape=pltpu.VMEM((seq_count, subs * group + owned, LANES), f32),
        scratch_shapes=[
            pltpu.VMEM((seq_count * (subs * group + 1), LANES), f32),
            pltpu.VMEM((2 * group * seq_count * subs, 4 * LANES), bf16),
            pltpu.VMEM((group * seq_count * subs, 4 * LANES), bf16),
            pltpu.VMEM((2 * group * seq_count * subs, 2 * LANES), bf16),
            pltpu.VMEM((seq_count * (2 * subs * group + 1), LANES), f32),
        ],
        interpret=INTERPRET,
        name="conv",
        compiler_params=pltpu.CompilerParams(vmem_limit_bytes=VMEM_LIMIT),
    )(taken, in_vmem(bounds), in_vmem(row_sizes), in_vmem(table))
    back = lax.all_to_all(mixed_sent, "seq", 0, 0)
    back = in_vmem(back)
    return pl.pallas_call(
        functools.partial(back_kernel, **sizes),
        out_shape=(
            jax.ShapeDtypeStruct((block_rows, channels), f32),
            jax.ShapeDtypeStruct((owned, channels), f32),
        ),
        interpret=INTERPRET,
        name="back",
        compiler_params=pltpu.CompilerParams(vmem_limit_bytes=VMEM_LIMIT),
    )(back)


def solution(mesh):
    placed = (P("seq", "chan"), P("seq", "chan"), P("seq", "chan"), P("chan"), P(), P())
    return jax.shard_map(
        on_device,
        mesh=mesh,
        in_specs=placed,
        out_specs=(P("seq", "chan"), P("seq", "chan")),
        check_vma=False,
    )
```

time: 54.3 us -> 50.9 us (0.937)
  Pallas kernels: 9.34 us -> 6.01 us
    pallas_call x1, Pallas kernels: 6.53 us -> 2.94 us  [on_device(): pl.pallas_call(functools.partial(conv_kernel, **sizes), out_shape=pltpu.V...]
where the time goes in v4:
time: 50.9 us; the launch traced here: 50.7 us
  blocking collectives  44.1 us (87%)
  Pallas kernels  6.01 us (12%)
  between operations  0.64 us (1%)
    all_to_all x1, blocking collectives, on_device(): taken = lax.all_to_all(sent, 'seq', 0, 0)  29.6 us
    all_to_all x1, blocking collectives, on_device(): back = lax.all_to_all(mixed_sent, 'seq', 0, 0)  14.5 us
    pallas_call x1, Pallas kernels, on_device(): pl.pallas_call(functools.partial(conv_kernel, **sizes), out_shape=pltpu.V...  2.94 us
    pallas_call x1, Pallas kernels, on_device(): pl.pallas_call(functools.partial(turn_kernel, **sizes), in_specs=[anywher...  2.08 us

profile of v4, /device:TPU:96, one launch (start us, length us, event | category | flops | bytes accessed | tf_op | source)
XLA Modules:
  0.0 50.7 jit_solution(6771729173832597201)
XLA Ops:
  0.6 2.1 %turn.1 = (f32[16,192,128]{2,1,0:T(8,128)S(1)}, f32[32,128]{1,0:T(8,128)S(1)}, f32[32,128]{1,0:T(8,128)S(1)}, bf16[1472,256]{1,0:T(8,128)(2,1)S(1)}) custom-call(f32[512,256]{1,0:T(8,128)} %signal.1, f32[512,256]{1,0:T(8,128)} %taps.1, f32[512,256]{1,0:T(8,128)} %gate.1, f32[1,256]{1,0:T(1,128)} %bitcast.5, s32[1,128]{1,0:T(1,128)} %bitcast.6, ...), custom_call_target="tpu_custom_call" | custom-call | tf_op jit(solution)/shard_map/turn/pallas_call | solution.py:268
  2.7 29.6 %all_to_all.10 = f32[16,192,128]{2,1,0:T(8,128)S(1)} all-to-all(f32[16,192,128]{2,1,0:T(8,128)S(1)} %get-tuple-element.6), channel_id=1, replica_groups=mesh['seq'=16,'chan'=16] {'seq'}, dimensions={0} | all-to-all | bytes 3145728 | tf_op jit(solution)/shard_map/all_to_all | solution.py:301
  32.3 2.9 %conv.1 = f32[16,72,128]{2,1,0:T(8,128)S(1)} custom-call(f32[3072,128]{1,0:T(8,128)S(1)} %bitcast.4, f32[32,128]{1,0:T(8,128)S(1)} %get-tuple-element.7.bounds, f32[32,128]{1,0:T(8,128)S(1)} %get-tuple-element.8.sizes, bf16[1472,256]{1,0:T(8,128)(2,1)S(1)} %get-tuple-element.9.table), custom_call_target="tpu_custom_call" | custom-call | tf_op jit(solution)/shard_map/conv/pallas_call | solution.py:303
  35.3 14.5 %all_to_all.11.taken = f32[16,72,128]{2,1,0:T(8,128)S(1)} all-to-all(f32[16,72,128]{2,1,0:T(8,128)S(1)} %conv.1), channel_id=1, replica_groups=mesh['seq'=16,'chan'=16] {'seq'}, dimensions={0} | all-to-all | bytes 1179648 | tf_op jit(solution)/shard_map/all_to_all | solution.py:317
  49.7 1.0 %back.1 = (f32[512,256]{1,0:T(8,128)}, f32[8,256]{1,0:T(8,128)}) custom-call(f32[16,72,128]{2,1,0:T(8,128)S(1)} %all_to_all.11.taken), custom_call_target="tpu_custom_call" | custom-call | tf_op jit(solution)/shard_map/back/pallas_call | solution.py:319

commit v5 on v4

--- a/solution.py
+++ b/solution.py
@@ -16,8 +16,26 @@
 ACC = 2
 INV = 4
 INTERPRET = False
+OUT_ORDER = [10, 6, 12, 2, 13, 4, 5, 7, 3, 0, 9, 14, 15, 8, 1, 11]
+BACK_ORDER = OUT_ORDER
 bf16 = jnp.bfloat16
 f32 = jnp.float32
+
+
+def order_of(wanted, seq_count):
+    return wanted if len(wanted) == seq_count else list(range(seq_count))
+
+
+def exchange(value, order):
+    return lax.all_to_all(value, "seq", 0, 0, axis_index_groups=[order])
+
+
+def place_in(order):
+    mine = lax.axis_index("seq")
+    place = jnp.int32(0)
+    for at, device in enumerate(order):
+        place = jnp.where(mine == device, at, place)
+    return place
 
 
 def split_const(value):
@@ -29,7 +47,8 @@
 def tables(seq_count, subs):
     rows = seq_count * subs
     total = rows * LANES
-    t1 = np.array([device * subs + sub for sub in range(subs) for device in range(seq_count)], np.float64)
+    order = order_of(OUT_ORDER, seq_count)
+    t1 = np.array([device * subs + sub for sub in range(subs) for device in order], np.float64)
     k1 = np.arange(rows, dtype=np.float64)
     t2 = np.arange(LANES, dtype=np.float64)
     first = -2.0 * math.pi * (k1[:, None] + 0.25) * t1[None, :] / rows
@@ -39,14 +58,13 @@
     cos, sin = np.cos(angle), np.sin(angle)
     forward = np.block([[cos, -sin], [sin, cos]])
     last = 2.0 * math.pi * t1[:, None] * (k1[None, :] + 0.25) / rows
-    last_hi, last_lo = split_const(np.concatenate([np.cos(last), -np.sin(last)], 1))
+    last_hi, last_lo = split_const(np.concatenate([np.cos(last), np.sin(last)], 1) / total)
     twist = -2.0 * math.pi * (k1[:, None] + 0.25) * t2[None, :] / total
     twist = np.concatenate([np.cos(twist), np.sin(twist)], 1)
     high, middle = split_const(twist)
     low = (twist - high.astype(np.float64) - middle.astype(np.float64)).astype(bf16)
     parts = [
         *split_const(forward),
-        *split_const(forward.T / total),
         first3,
         np.concatenate([last_hi, last_lo], 1),
         np.concatenate([last_hi, np.zeros_like(last_hi)], 1),
@@ -82,11 +100,8 @@
     constant = pltpu.make_async_copy(consts, table, small_sems.at[3])
     large = []
     for which, ref in enumerate((signal, taps, gate)):
-        for sub in range(subs):
-            rows = pl.ds(sub * LANES, LANES)
-            at = which * subs + sub
-            large.append(pltpu.make_async_copy(ref.at[rows, :], big.at[at], sems.at[at]))
-            large[-1].start()
+        large.append(pltpu.make_async_copy(ref, big.at[which], sems.at[which]))
+        large[-1].start()
     constant.start()
     for copy in small:
         copy.wait()
@@ -104,10 +119,9 @@
 
     at_start = lax.axis_index("seq") == 0
     for which in range(3):
+        large[which].wait()
         for sub in range(subs):
-            large[which * subs + sub].wait()
-        for sub in range(subs):
-            value = big[which * subs + sub]
+            value = big[which, sub * LANES : (sub + 1) * LANES, :]
             if which == 1 and sub == 0:
                 place = lax.broadcasted_iota(jnp.int32, value.shape, 0)
                 value = value + jnp.where((place == 0) & at_start, row[...], 0.0)
@@ -126,7 +140,7 @@
     def tabled(at, count, lanes=wide):
         return table[at : at + count, :lanes]
 
-    at = 4 * wide
+    at = 2 * wide
     first3 = tabled(at, 2 * rows, 3 * rows)
     at += 2 * rows
     last3 = jnp.concatenate([tabled(at, rows), tabled(at + rows, rows, LANES)], 1)
@@ -164,19 +178,19 @@
                 turned[at, lanes_out] = hi
                 turned[at, 2 * LANES + half * LANES : 2 * LANES + (half + 1) * LANES] = lo
 
-    def three(ref, at, base):
-        high, low = tabled(base, wide), tabled(base + wide, wide)
+    def three(ref, at):
+        high, low = tabled(0, wide), tabled(wide, wide)
         return mm(jnp.concatenate([ref[at, :], ref[at, :wide]], 1), jnp.concatenate([high, high, low], 0))
 
     for block in range(group // FWD):
-        spec = three(turned, slice(block * FWD * 2 * rows, (block + 1) * FWD * 2 * rows), 0)
+        spec = three(turned, slice(block * FWD * 2 * rows, (block + 1) * FWD * 2 * rows))
         for at in range(FWD):
             channel = block * FWD + at
             left = spec[(2 * at) * rows : (2 * at + 1) * rows]
             right = spec[(2 * at + 1) * rows : (2 * at + 2) * rows]
             left_re, left_im = left[:, :LANES], left[:, LANES:]
             right_re, right_im = right[:, :LANES], right[:, LANES:]
-            products = (left_re * right_re - left_im * right_im, left_re * right_im + left_im * right_re)
+            products = (left_re * right_re - left_im * right_im, -(left_re * right_im) - left_im * right_re)
             here = slice(channel * rows, (channel + 1) * rows)
             for half, value in enumerate(products):
                 hi, lo = split(value)
@@ -184,12 +198,12 @@
                 product[here, (2 + half) * LANES : (3 + half) * LANES] = lo
 
     for block in range(group // INV):
-        back = three(product, slice(block * INV * rows, (block + 1) * INV * rows), 2 * wide)
+        back = three(product, slice(block * INV * rows, (block + 1) * INV * rows))
         for at in range(INV):
             channel = block * INV + at
             lanes = slice(channel % 2 * LANES, (channel % 2 + 1) * LANES)
             re, im = back[at * rows : (at + 1) * rows, :LANES], back[at * rows : (at + 1) * rows, LANES:]
-            values = (re * twist_re + im * twist_im, im * twist_re - re * twist_im)
+            values = (re * twist_re - im * twist_im, im * twist_re + re * twist_im)
             for half, value in enumerate(values):
                 hi, lo = split(value)
                 base = channel // 2 * 4 * rows + half * rows
@@ -214,39 +228,43 @@
     past_start = past_start.astype(jnp.int16)
     one, zero = jnp.ones((wide, segs), bf16), jnp.zeros((wide, segs), bf16)
     sums = [jnp.zeros((2 * group, segs), f32) for _ in range(ACC)]
-    for device in range(seq_count):
+    arrived, leaving = order_of(OUT_ORDER, seq_count), order_of(BACK_ORDER, seq_count)
+    for at, device in enumerate(arrived):
         for step in range(subs // 2):
             halves = []
             for sub in (2 * step, 2 * step + 1):
-                base = device * (subs * group + 1) + sub * group
-                from_row = device * per + (sub * 3 + 2) * group
+                base = at * (subs * group + 1) + sub * group
+                from_row = at * per + (sub * 3 + 2) * group
                 mixed = conv[base : base + group, :] * taken[from_row : from_row + group, :]
-                out[device, sub * group : (sub + 1) * group, :] = mixed
+                out[leaving.index(device), sub * group : (sub + 1) * group, :] = mixed
                 halves.append(mixed)
             hi, lo = split(jnp.concatenate(halves, 1))
             offset = (device * subs + 2 * step) * LANES
             member = jnp.where(
                 (past_start >= jnp.int16(-offset)) & (to_end >= jnp.int16(offset)), one, zero
             )
-            which = (device * (subs // 2) + step) % ACC
+            which = (at * (subs // 2) + step) % ACC
             sums[which] = sums[which] + mm(jnp.concatenate([hi, lo], 0), member)
     acc = sum(sums[1:], sums[0])
     pooled = (acc[:group] + acc[group:]) / sizes[:group, :]
     pooled = jnp.concatenate([pooled, jnp.zeros((LANES - group, segs), f32)], 0).T
-    shift = lax.rem(lax.axis_index("seq"), LANES // group) * group
+    shift = lax.rem(place_in(arrived), LANES // group) * group
     pooled = pltpu.roll(pooled, shift, 1)
-    out[:, subs * group :, :] = pooled.reshape(seq_count, owned, LANES)
+    for at, device in enumerate(leaving):
+        out[at, subs * group :, :] = pooled[device * owned : (device + 1) * owned, :]
 
 
 def back_kernel(taken, mixed, pooled, *, seq_count, group, subs):
     channels = seq_count * group
+    leaving = order_of(BACK_ORDER, seq_count)
+    holder = [leaving.index(device) for device in order_of(OUT_ORDER, seq_count)]
     for sub in range(subs):
-        block = taken[:, sub * group : (sub + 1) * group, :].reshape(channels, LANES)
+        block = jnp.concatenate([taken[at, sub * group : (sub + 1) * group, :] for at in holder], 0)
         mixed[sub * LANES : (sub + 1) * LANES, :] = block.T
     per_lane = LANES // group
     for half in range(channels // LANES):
-        total = taken[half * per_lane, subs * group :, :]
-        for at in range(half * per_lane + 1, (half + 1) * per_lane):
+        total = taken[holder[half * per_lane], subs * group :, :]
+        for at in holder[half * per_lane + 1 : (half + 1) * per_lane]:
             total = total + taken[at, subs * group :, :]
         pooled[:, half * LANES : (half + 1) * LANES] = total
 
@@ -275,7 +293,7 @@
             pltpu.VMEM(consts.shape, bf16),
         ),
         scratch_shapes=[
-            pltpu.VMEM((3 * subs, LANES, channels), f32),
+            pltpu.VMEM((3, subs * LANES, channels), f32),
             pltpu.VMEM((1, channels), f32),
             pltpu.VMEM((2, 1, segs), jnp.int32),
             pltpu.SemaphoreType.DMA((3 * subs,)),
@@ -298,7 +316,7 @@
             )
         )
     )
-    taken = lax.all_to_all(sent, "seq", 0, 0)
+    taken = exchange(sent, order_of(OUT_ORDER, seq_count))
     taken = in_vmem(taken.reshape(seq_count * 3 * subs * group, LANES))
     mixed_sent = pl.pallas_call(
         functools.partial(conv_kernel, **sizes),
@@ -314,7 +332,7 @@
         name="conv",
         compiler_params=pltpu.CompilerParams(vmem_limit_bytes=VMEM_LIMIT),
     )(taken, in_vmem(bounds), in_vmem(row_sizes), in_vmem(table))
-    back = lax.all_to_all(mixed_sent, "seq", 0, 0)
+    back = exchange(mixed_sent, order_of(BACK_ORDER, seq_count))
     back = in_vmem(back)
     return pl.pallas_call(
         functools.partial(back_kernel, **sizes),

time: 50.9 us -> 47 us (0.923)
  blocking collectives: 44.1 us -> 40.3 us
    all_to_all x2, blocking collectives: 44.1 us -> 40.3 us  [exchange(): return lax.all_to_all(value, 'seq', 0, 0, axis_index_groups=[order])]
where the time goes in v5:
time: 47 us; the launch traced here: 46.8 us
  blocking collectives  40.3 us (86%)
  Pallas kernels  5.8 us (12%)
  between operations  0.64 us (1%)
    all_to_all x2, blocking collectives, exchange(): return lax.all_to_all(value, 'seq', 0, 0, axis_index_groups=[order])  40.3 us
    pallas_call x1, Pallas kernels, on_device(): pl.pallas_call(functools.partial(conv_kernel, **sizes), out_shape=pltpu.V...  2.97 us
    pallas_call x1, Pallas kernels, on_device(): pl.pallas_call(functools.partial(turn_kernel, **sizes), in_specs=[anywher...  1.83 us
    pallas_call x1, Pallas kernels, on_device(): pl.pallas_call(functools.partial(back_kernel, **sizes), out_shape=(jax.Sh...  1 us

profile of v5, /device:TPU:96, one launch (start us, length us, event | category | flops | bytes accessed | tf_op | source)
XLA Modules:
  0.0 46.8 jit_solution(3525709816222862799)
XLA Ops:
  0.6 1.8 %turn.1 = (f32[16,192,128]{2,1,0:T(8,128)S(1)}, f32[32,128]{1,0:T(8,128)S(1)}, f32[32,128]{1,0:T(8,128)S(1)}, bf16[960,256]{1,0:T(8,128)(2,1)S(1)}) custom-call(f32[512,256]{1,0:T(8,128)} %signal.1, f32[512,256]{1,0:T(8,128)} %taps.1, f32[512,256]{1,0:T(8,128)} %gate.1, f32[1,256]{1,0:T(1,128)} %bitcast.5, s32[1,128]{1,0:T(1,128)} %bitcast.6, ...), custom_call_target="tpu_custom_call" | custom-call | tf_op jit(solution)/shard_map/turn/pallas_call | solution.py:286
  2.5 26.4 %all_to_all.10 = f32[16,192,128]{2,1,0:T(8,128)S(1)} all-to-all(f32[16,192,128]{2,1,0:T(8,128)S(1)} %get-tuple-element.6), channel_id=1, replica_groups={{160,96,192,32,208,64,80,112,48,0,144,224,240,128,16,176},{161,97,193,3..., dimensions={0} | all-to-all | bytes 3145728 | tf_op jit(solution)/shard_map/all_to_all | solution.py:30
  28.9 3.0 %conv.1 = f32[16,72,128]{2,1,0:T(8,128)S(1)} custom-call(f32[3072,128]{1,0:T(8,128)S(1)} %bitcast.4, f32[32,128]{1,0:T(8,128)S(1)} %get-tuple-element.7.bounds, f32[32,128]{1,0:T(8,128)S(1)} %get-tuple-element.8.sizes, bf16[960,256]{1,0:T(8,128)(2,1)S(1)} %get-tuple-element.9.table), custom_call_target="tpu_custom_call" | custom-call | tf_op jit(solution)/shard_map/conv/pallas_call | solution.py:321
  31.8 13.9 %all_to_all.11.taken = f32[16,72,128]{2,1,0:T(8,128)S(1)} all-to-all(f32[16,72,128]{2,1,0:T(8,128)S(1)} %conv.1), channel_id=1, replica_groups={{160,96,192,32,208,64,80,112,48,0,144,224,240,128,16,176},{161,97,193,3..., dimensions={0} | all-to-all | bytes 1179648 | tf_op jit(solution)/shard_map/all_to_all | solution.py:30
  45.8 1.0 %back.1 = (f32[512,256]{1,0:T(8,128)}, f32[8,256]{1,0:T(8,128)}) custom-call(f32[16,72,128]{2,1,0:T(8,128)S(1)} %all_to_all.11.taken), custom_call_target="tpu_custom_call" | custom-call | tf_op jit(solution)/shard_map/back/pallas_call | solution.py:337

commit v6 on v5

--- a/solution.py
+++ b/solution.py
@@ -16,7 +16,7 @@
 ACC = 2
 INV = 4
 INTERPRET = False
-OUT_ORDER = [10, 6, 12, 2, 13, 4, 5, 7, 3, 0, 9, 14, 15, 8, 1, 11]
+OUT_ORDER = [10, 11, 5, 2, 7, 4, 12, 9, 8, 3, 1, 14, 13, 0, 15, 6]
 BACK_ORDER = OUT_ORDER
 bf16 = jnp.bfloat16
 f32 = jnp.float32
@@ -254,19 +254,27 @@
         out[at, subs * group :, :] = pooled[device * owned : (device + 1) * owned, :]
 
 
-def back_kernel(taken, mixed, pooled, *, seq_count, group, subs):
+def back_kernel(taken, mixed, pooled, turned, summed, sems, *, seq_count, group, subs):
     channels = seq_count * group
     leaving = order_of(BACK_ORDER, seq_count)
     holder = [leaving.index(device) for device in order_of(OUT_ORDER, seq_count)]
+    copies = []
     for sub in range(subs):
         block = jnp.concatenate([taken[at, sub * group : (sub + 1) * group, :] for at in holder], 0)
-        mixed[sub * LANES : (sub + 1) * LANES, :] = block.T
+        turned[sub] = block.T
+        rows = pl.ds(sub * LANES, LANES)
+        copies.append(pltpu.make_async_copy(turned.at[sub], mixed.at[rows, :], sems.at[sub]))
+        copies[-1].start()
     per_lane = LANES // group
     for half in range(channels // LANES):
         total = taken[holder[half * per_lane], subs * group :, :]
         for at in holder[half * per_lane + 1 : (half + 1) * per_lane]:
             total = total + taken[at, subs * group :, :]
-        pooled[:, half * LANES : (half + 1) * LANES] = total
+        summed[:, half * LANES : (half + 1) * LANES] = total
+    copies.append(pltpu.make_async_copy(summed, pooled, sems.at[subs]))
+    copies[-1].start()
+    for copy in copies:
+        copy.wait()
 
 
 def in_vmem(value):
@@ -340,6 +348,12 @@
             jax.ShapeDtypeStruct((block_rows, channels), f32),
             jax.ShapeDtypeStruct((owned, channels), f32),
         ),
+        out_specs=(pl.BlockSpec(memory_space=pltpu.HBM), pl.BlockSpec(memory_space=pltpu.HBM)),
+        scratch_shapes=[
+            pltpu.VMEM((subs, LANES, channels), f32),
+            pltpu.VMEM((owned, channels), f32),
+            pltpu.SemaphoreType.DMA((subs + 1,)),
+        ],
         interpret=INTERPRET,
         name="back",
         compiler_params=pltpu.CompilerParams(vmem_limit_bytes=VMEM_LIMIT),

time: 47 us -> 46.3 us (0.985)
  blocking collectives: 40.3 us -> 39.7 us
    all_to_all x2, blocking collectives: 40.3 us -> 39.7 us  [exchange(): return lax.all_to_all(value, 'seq', 0, 0, axis_index_groups=[order])]
where the time goes in v6:
time: 46.3 us; the launch traced here: 46.1 us
  blocking collectives  39.7 us (86%)
  Pallas kernels  5.71 us (12%)
  between operations  0.64 us (1%)
    all_to_all x2, blocking collectives, exchange(): return lax.all_to_all(value, 'seq', 0, 0, axis_index_groups=[order])  39.7 us
    pallas_call x1, Pallas kernels, on_device(): pl.pallas_call(functools.partial(conv_kernel, **sizes), out_shape=pltpu.V...  2.95 us
    pallas_call x1, Pallas kernels, on_device(): pl.pallas_call(functools.partial(turn_kernel, **sizes), in_specs=[anywher...  1.83 us
    pallas_call x1, Pallas kernels, on_device(): pl.pallas_call(functools.partial(back_kernel, **sizes), out_shape=(jax.Sh...  0.93 us

profile of v6, /device:TPU:96, one launch (start us, length us, event | category | flops | bytes accessed | tf_op | source)
XLA Modules:
  0.0 46.1 jit_solution(2306228171037446326)
XLA Ops:
  0.6 1.8 %turn.1 = (f32[16,192,128]{2,1,0:T(8,128)S(1)}, f32[32,128]{1,0:T(8,128)S(1)}, f32[32,128]{1,0:T(8,128)S(1)}, bf16[960,256]{1,0:T(8,128)(2,1)S(1)}) custom-call(f32[512,256]{1,0:T(8,128)} %signal.1, f32[512,256]{1,0:T(8,128)} %taps.1, f32[512,256]{1,0:T(8,128)} %gate.1, f32[1,256]{1,0:T(1,128)} %bitcast.5, s32[1,128]{1,0:T(1,128)} %bitcast.6, ...), custom_call_target="tpu_custom_call" | custom-call | tf_op jit(solution)/shard_map/turn/pallas_call | solution.py:294
  2.5 26.7 %all_to_all.10 = f32[16,192,128]{2,1,0:T(8,128)S(1)} all-to-all(f32[16,192,128]{2,1,0:T(8,128)S(1)} %get-tuple-element.6), channel_id=1, replica_groups={{160,176,80,32,112,64,192,144,128,48,16,224,208,0,240,96},{161,177,81,3..., dimensions={0} | all-to-all | bytes 3145728 | tf_op jit(solution)/shard_map/all_to_all | solution.py:30
  29.2 3.0 %conv.1 = f32[16,72,128]{2,1,0:T(8,128)S(1)} custom-call(f32[3072,128]{1,0:T(8,128)S(1)} %bitcast.4, f32[32,128]{1,0:T(8,128)S(1)} %get-tuple-element.7.bounds, f32[32,128]{1,0:T(8,128)S(1)} %get-tuple-element.8.sizes, bf16[960,256]{1,0:T(8,128)(2,1)S(1)} %get-tuple-element.9.table), custom_call_target="tpu_custom_call" | custom-call | tf_op jit(solution)/shard_map/conv/pallas_call | solution.py:329
  32.2 13.0 %all_to_all.11.taken = f32[16,72,128]{2,1,0:T(8,128)S(1)} all-to-all(f32[16,72,128]{2,1,0:T(8,128)S(1)} %conv.1), channel_id=1, replica_groups={{160,176,80,32,112,64,192,144,128,48,16,224,208,0,240,96},{161,177,81,3..., dimensions={0} | all-to-all | bytes 1179648 | tf_op jit(solution)/shard_map/all_to_all | solution.py:30
  45.2 0.9 %back.1 = (f32[512,256]{1,0:T(8,128)}, f32[8,256]{1,0:T(8,128)}) custom-call(f32[16,72,128]{2,1,0:T(8,128)S(1)} %all_to_all.11.taken), custom_call_target="tpu_custom_call" | custom-call | tf_op jit(solution)/shard_map/back/pallas_call | solution.py:345

commit v7 on v6

--- a/solution.py
+++ b/solution.py
@@ -95,13 +95,13 @@
         pltpu.make_async_copy(row_of, ints.at[1], small_sems.at[1]),
         pltpu.make_async_copy(skip, row, small_sems.at[2]),
     )
-    for copy in small:
-        copy.start()
     constant = pltpu.make_async_copy(consts, table, small_sems.at[3])
     large = []
     for which, ref in enumerate((signal, taps, gate)):
         large.append(pltpu.make_async_copy(ref, big.at[which], sems.at[which]))
         large[-1].start()
+    for copy in small:
+        copy.start()
     constant.start()
     for copy in small:
         copy.wait()

time: 46.3 us -> 46.3 us (level)
  no operation moved by 1% of the time
where the time goes in v7:
time: 46.3 us; the launch traced here: 46.2 us
  blocking collectives  39.7 us (86%)
  Pallas kernels  5.8 us (13%)
  between operations  0.64 us (1%)
    all_to_all x2, blocking collectives, exchange(): return lax.all_to_all(value, 'seq', 0, 0, axis_index_groups=[order])  39.7 us
    pallas_call x1, Pallas kernels, on_device(): pl.pallas_call(functools.partial(conv_kernel, **sizes), out_shape=pltpu.V...  2.95 us
    pallas_call x1, Pallas kernels, on_device(): pl.pallas_call(functools.partial(turn_kernel, **sizes), in_specs=[anywher...  1.92 us
    pallas_call x1, Pallas kernels, on_device(): pl.pallas_call(functools.partial(back_kernel, **sizes), out_shape=(jax.Sh...  0.93 us

profile of v7, /device:TPU:96, one launch (start us, length us, event | category | flops | bytes accessed | tf_op | source)
XLA Modules:
  0.0 46.2 jit_solution(2840717126058510559)
XLA Ops:
  0.6 1.9 %turn.1 = (f32[16,192,128]{2,1,0:T(8,128)S(1)}, f32[32,128]{1,0:T(8,128)S(1)}, f32[32,128]{1,0:T(8,128)S(1)}, bf16[960,256]{1,0:T(8,128)(2,1)S(1)}) custom-call(f32[512,256]{1,0:T(8,128)} %signal.1, f32[512,256]{1,0:T(8,128)} %taps.1, f32[512,256]{1,0:T(8,128)} %gate.1, f32[1,256]{1,0:T(1,128)} %bitcast.5, s32[1,128]{1,0:T(1,128)} %bitcast.6, ...), custom_call_target="tpu_custom_call" | custom-call | tf_op jit(solution)/shard_map/turn/pallas_call | solution.py:294
  2.6 26.7 %all_to_all.10 = f32[16,192,128]{2,1,0:T(8,128)S(1)} all-to-all(f32[16,192,128]{2,1,0:T(8,128)S(1)} %get-tuple-element.6), channel_id=1, replica_groups={{160,176,80,32,112,64,192,144,128,48,16,224,208,0,240,96},{161,177,81,3..., dimensions={0} | all-to-all | bytes 3145728 | tf_op jit(solution)/shard_map/all_to_all | solution.py:30
  29.3 3.0 %conv.1 = f32[16,72,128]{2,1,0:T(8,128)S(1)} custom-call(f32[3072,128]{1,0:T(8,128)S(1)} %bitcast.4, f32[32,128]{1,0:T(8,128)S(1)} %get-tuple-element.7.bounds, f32[32,128]{1,0:T(8,128)S(1)} %get-tuple-element.8.sizes, bf16[960,256]{1,0:T(8,128)(2,1)S(1)} %get-tuple-element.9.table), custom_call_target="tpu_custom_call" | custom-call | tf_op jit(solution)/shard_map/conv/pallas_call | solution.py:329
  32.2 13.0 %all_to_all.11.taken = f32[16,72,128]{2,1,0:T(8,128)S(1)} all-to-all(f32[16,72,128]{2,1,0:T(8,128)S(1)} %conv.1), channel_id=1, replica_groups={{160,176,80,32,112,64,192,144,128,48,16,224,208,0,240,96},{161,177,81,3..., dimensions={0} | all-to-all | bytes 1179648 | tf_op jit(solution)/shard_map/all_to_all | solution.py:30
  45.2 0.9 %back.1 = (f32[512,256]{1,0:T(8,128)}, f32[8,256]{1,0:T(8,128)}) custom-call(f32[16,72,128]{2,1,0:T(8,128)S(1)} %all_to_all.11.taken), custom_call_target="tpu_custom_call" | custom-call | tf_op jit(solution)/shard_map/back/pallas_call | solution.py:345

commit v8 on v7

--- a/solution.py
+++ b/solution.py
@@ -259,12 +259,6 @@
     leaving = order_of(BACK_ORDER, seq_count)
     holder = [leaving.index(device) for device in order_of(OUT_ORDER, seq_count)]
     copies = []
-    for sub in range(subs):
-        block = jnp.concatenate([taken[at, sub * group : (sub + 1) * group, :] for at in holder], 0)
-        turned[sub] = block.T
-        rows = pl.ds(sub * LANES, LANES)
-        copies.append(pltpu.make_async_copy(turned.at[sub], mixed.at[rows, :], sems.at[sub]))
-        copies[-1].start()
     per_lane = LANES // group
     for half in range(channels // LANES):
         total = taken[holder[half * per_lane], subs * group :, :]
@@ -273,6 +267,12 @@
         summed[:, half * LANES : (half + 1) * LANES] = total
     copies.append(pltpu.make_async_copy(summed, pooled, sems.at[subs]))
     copies[-1].start()
+    for sub in range(subs):
+        block = jnp.concatenate([taken[at, sub * group : (sub + 1) * group, :] for at in holder], 0)
+        turned[sub] = block.T
+        rows = pl.ds(sub * LANES, LANES)
+        copies.append(pltpu.make_async_copy(turned.at[sub], mixed.at[rows, :], sems.at[sub]))
+        copies[-1].start()
     for copy in copies:
         copy.wait()
 

time: 46.3 us -> 46.3 us (level)
  no operation moved by 1% of the time
where the time goes in v8:
time: 46.3 us; the launch traced here: 46.2 us
  blocking collectives  39.7 us (86%)
  Pallas kernels  5.8 us (13%)
  between operations  0.64 us (1%)
    all_to_all x2, blocking collectives, exchange(): return lax.all_to_all(value, 'seq', 0, 0, axis_index_groups=[order])  39.7 us
    pallas_call x1, Pallas kernels, on_device(): pl.pallas_call(functools.partial(conv_kernel, **sizes), out_shape=pltpu.V...  2.95 us
    pallas_call x1, Pallas kernels, on_device(): pl.pallas_call(functools.partial(turn_kernel, **sizes), in_specs=[anywher...  1.92 us
    pallas_call x1, Pallas kernels, on_device(): pl.pallas_call(functools.partial(back_kernel, **sizes), out_shape=(jax.Sh...  0.93 us

profile of v8, /device:TPU:96, one launch (start us, length us, event | category | flops | bytes accessed | tf_op | source)
XLA Modules:
  0.0 46.2 jit_solution(3188901025628325263)
XLA Ops:
  0.6 1.9 %turn.1 = (f32[16,192,128]{2,1,0:T(8,128)S(1)}, f32[32,128]{1,0:T(8,128)S(1)}, f32[32,128]{1,0:T(8,128)S(1)}, bf16[960,256]{1,0:T(8,128)(2,1)S(1)}) custom-call(f32[512,256]{1,0:T(8,128)} %signal.1, f32[512,256]{1,0:T(8,128)} %taps.1, f32[512,256]{1,0:T(8,128)} %gate.1, f32[1,256]{1,0:T(1,128)} %bitcast.5, s32[1,128]{1,0:T(1,128)} %bitcast.6, ...), custom_call_target="tpu_custom_call" | custom-call | tf_op jit(solution)/shard_map/turn/pallas_call | solution.py:294
  2.6 26.7 %all_to_all.10 = f32[16,192,128]{2,1,0:T(8,128)S(1)} all-to-all(f32[16,192,128]{2,1,0:T(8,128)S(1)} %get-tuple-element.6), channel_id=1, replica_groups={{160,176,80,32,112,64,192,144,128,48,16,224,208,0,240,96},{161,177,81,3..., dimensions={0} | all-to-all | bytes 3145728 | tf_op jit(solution)/shard_map/all_to_all | solution.py:30
  29.3 3.0 %conv.1 = f32[16,72,128]{2,1,0:T(8,128)S(1)} custom-call(f32[3072,128]{1,0:T(8,128)S(1)} %bitcast.4, f32[32,128]{1,0:T(8,128)S(1)} %get-tuple-element.7.bounds, f32[32,128]{1,0:T(8,128)S(1)} %get-tuple-element.8.sizes, bf16[960,256]{1,0:T(8,128)(2,1)S(1)} %get-tuple-element.9.table), custom_call_target="tpu_custom_call" | custom-call | tf_op jit(solution)/shard_map/conv/pallas_call | solution.py:329
  32.2 13.0 %all_to_all.11.taken = f32[16,72,128]{2,1,0:T(8,128)S(1)} all-to-all(f32[16,72,128]{2,1,0:T(8,128)S(1)} %conv.1), channel_id=1, replica_groups={{160,176,80,32,112,64,192,144,128,48,16,224,208,0,240,96},{161,177,81,3..., dimensions={0} | all-to-all | bytes 1179648 | tf_op jit(solution)/shard_map/all_to_all | solution.py:30
  45.2 0.9 %back.1 = (f32[512,256]{1,0:T(8,128)}, f32[8,256]{1,0:T(8,128)}) custom-call(f32[16,72,128]{2,1,0:T(8,128)S(1)} %all_to_all.11.taken), custom_call_target="tpu_custom_call" | custom-call | tf_op jit(solution)/shard_map/back/pallas_call | solution.py:345
